TPU v7x, 512 devices: a whole 4x8x8 slice. The times are simulated.
512 devices in a mesh: edge: 32 (over x, z), feat: 16 (over y, core).
Axes of the slice: x: 4, y: 8, z: 8, core: 2. Of those that a mesh axis runs over, the one named last changes fastest.
Arguments:
- features: bfloat16 [16384, 2048], P('edge', 'feat'), may hold values from -6 to 6
- tiles: bfloat16 [1536, 128, 128], P('edge'), may hold values from -0.0546875 to 0.0546875
- tile_slot: int32 [12288], P('edge'), may hold values from 0 to 127, as said below
- tile_col: int32 [12288], P('edge'), may hold values from 0 to 3, as said below
- tile_id: int32 [12288], P('edge'), may hold values from 0 to 47
- touched: int32 [32, 32, 4], replicated, may hold values from 0 to 3, as said below
- weight: bfloat16 [2048, 2048], P(None, 'feat'), may hold values from -0.125 to 0.125
- readers: int32 [512], P('edge'), may hold values from 0 to 127, as said below
Outputs:
- hidden: bfloat16 [16384, 2048], P('edge', 'feat')
- ghosts: bfloat16 [65536, 2048], P('edge', 'feat')
Inputs may be any that keep to these rules, and one draw needn't show every extreme that they name: For each sender and owner, the 4 entries of touched are distinct block numbers below 4. Within one device's 384 listed products, the pairs (tile_slot, tile_col) are all distinct. Within one device's 384 listed products, the pairs (tile_slot, tile_col) are all distinct. `readers`: one device's 16 entries are distinct, and at most 2 of them lie in the row blocks of any one index of edge; every device's list has some index of edge with exactly 2.
All inputs are finite; a program needn't handle non-finite values.
Results may differ from a plain program's by a relative error of at most 0.0049.
Values may be sent and summed in bfloat16 or wider, within the bound.
A program may use at most 128 MiB of HBM per device.

v0:
```python
import math

import jax
import jax.numpy as jnp
from jax import lax
from jax.sharding import PartitionSpec as P


def swapped(x, axis, stride):
    return lax.ppermute(x, axis, [(i, i ^ 1 << stride) for i in range(lax.axis_size(axis))])


def local(features, tiles, tile_slot, tile_col, tile_id, touched, weight, readers):
    edge_count = lax.axis_size("edge")
    my_index = lax.axis_index("edge")
    row_count, width = features.shape
    block_size = tiles.shape[1]
    local_blocks = row_count // block_size
    slot_cap = touched.shape[2]
    slot_total = edge_count * slot_cap
    inputs = features.reshape(local_blocks, block_size, width)
    tile_count = tile_slot.shape[0]
    per_step = math.gcd(tile_count, 64)

    def add_group(turn, partial_value):
        first_pos = turn * per_step
        slots = lax.dynamic_slice_in_dim(tile_slot, first_pos, per_step)
        columns = lax.dynamic_slice_in_dim(tile_col, first_pos, per_step)
        chosen = lax.dynamic_slice_in_dim(tile_id, first_pos, per_step)
        product = jnp.einsum(
            "gij,gjc->gic", tiles[chosen], inputs[columns], preferred_element_type=jnp.float32
        )
        return partial_value.at[slots].add(product)

    partial_value = lax.fori_loop(
        0,
        tile_count // per_step,
        add_group,
        jnp.zeros((slot_total, block_size, width), jnp.float32),
    )
    my_lists = lax.dynamic_index_in_dim(touched, my_index, 0, keepdims=False)
    owners = jnp.arange(slot_total, dtype=jnp.int32) // slot_cap
    dense = (
        jnp.zeros((edge_count, local_blocks, block_size, width), jnp.float32)
        .at[owners, my_lists.reshape(-1)]
        .add(partial_value)
    )
    for level in reversed(range(edge_count.bit_length() - 1)):
        paired = dense.reshape((2, dense.shape[0] // 2) + dense.shape[1:])
        my_bit = my_index >> level & 1
        kept = lax.dynamic_index_in_dim(paired, my_bit, 0, keepdims=False)
        outgoing = lax.dynamic_index_in_dim(paired, 1 - my_bit, 0, keepdims=False)
        dense = kept + swapped(outgoing, "edge", level)
    summed = dense[0]
    aggregated = summed.reshape(row_count, width).astype(jnp.bfloat16)
    mixed = jnp.dot(
        lax.all_gather(aggregated, "feat", axis=1, tiled=True),
        weight,
        preferred_element_type=jnp.float32,
    )
    hidden = jnp.maximum(mixed, 0.0).astype(jnp.bfloat16)
    read_count = readers.shape[0]
    piece_blocks = lax.all_gather(hidden, "edge", axis=0, tiled=True).reshape(-1, block_size, width)
    numbers = jnp.arange(piece_blocks.shape[0], dtype=jnp.int32)
    selector = (readers[:, None] == numbers[None, :]).astype(jnp.bfloat16)
    gathered = jnp.einsum("rn,nic->ric", selector, piece_blocks, preferred_element_type=jnp.float32)
    return (hidden, gathered.reshape(read_count * block_size, width).astype(jnp.bfloat16))


def solution(mesh):
    in_specs = (
        P("edge", "feat"),
        P("edge", None, None),
        P("edge"),
        P("edge"),
        P("edge"),
        P(),
        P(None, "feat"),
        P("edge"),
    )
    out_specs = (P("edge", "feat"), P("edge", "feat"))
    return jax.shard_map(local, mesh=mesh, in_specs=in_specs, out_specs=out_specs, check_vma=False)
```

profile of v0, /device:TPU:8, one launch (start us, length us, event | category | flops | bytes accessed | tf_op | source)
XLA Modules:
  0.0 591.5 jit_solution(976951874358012408)
XLA Ops:
  8.2 4.3 broadcast_in_dim.32
  12.5 144.2 %while.13 = (s32[]{:T(128)}, f32[128,128,128]{2,1,0:T(8,128)}, s32[384]{0:T(512)}, s32[384]{0:T(512)}, bf16[48,128,128]{2,1,0:T(8,128)(2,1)}, /*index=5*/s32[384...) while((s32[]{:T(128)}, f32[128,128,128]{2,1,0:T(8,128)}, ...), condition=%wide.region_2.0_spmd, body=%wide.region_0.0_spmd.sunk | while | flops 269486656 | bytes 29371300 | solution.py:35
  17.8 4.2 fusion.21
  22.8 13.7 %scatter_fusion = f32[128,128,128]{2,1,0:T(8,128)} fusion(f32[128,128,128]{2,1,0:T(8,128)} %get-tuple-element.202, s32[64]{0:T(128)S(1)} %compare_select_fusion.7, f32[64,128,128]{2,1,0:T(8,128)} %fusion.21), kind=kCustom, calls=%fused_computation.2.clone.1 | custom fusion | flops 1048576 | bytes 12583168 | tf_op jit(solution)/shard_map/while/body/eval_jaxpr/scatter-add | solution.py:33
  41.8 4.2 fusion.21
  46.8 13.7 %scatter_fusion = f32[128,128,128]{2,1,0:T(8,128)} fusion(f32[128,128,128]{2,1,0:T(8,128)} %get-tuple-element.202, s32[64]{0:T(128)S(1)} %compare_select_fusion.7, f32[64,128,128]{2,1,0:T(8,128)} %fusion.21), kind=kCustom, calls=%fused_computation.2.clone.1 | custom fusion | flops 1048576 | bytes 12583168 | tf_op jit(solution)/shard_map/while/body/eval_jaxpr/scatter-add | solution.py:33
  65.9 4.2 fusion.21
  70.9 13.7 %scatter_fusion = f32[128,128,128]{2,1,0:T(8,128)} fusion(f32[128,128,128]{2,1,0:T(8,128)} %get-tuple-element.202, s32[64]{0:T(128)S(1)} %compare_select_fusion.7, f32[64,128,128]{2,1,0:T(8,128)} %fusion.21), kind=kCustom, calls=%fused_computation.2.clone.1 | custom fusion | flops 1048576 | bytes 12583168 | tf_op jit(solution)/shard_map/while/body/eval_jaxpr/scatter-add | solution.py:33
  89.9 4.2 fusion.21
  94.8 13.8 %scatter_fusion = f32[128,128,128]{2,1,0:T(8,128)} fusion(f32[128,128,128]{2,1,0:T(8,128)} %get-tuple-element.202, s32[64]{0:T(128)S(1)} %compare_select_fusion.7, f32[64,128,128]{2,1,0:T(8,128)} %fusion.21), kind=kCustom, calls=%fused_computation.2.clone.1 | custom fusion | flops 1048576 | bytes 12583168 | tf_op jit(solution)/shard_map/while/body/eval_jaxpr/scatter-add | solution.py:33
  113.9 4.2 fusion.21
  118.9 13.7 %scatter_fusion = f32[128,128,128]{2,1,0:T(8,128)} fusion(f32[128,128,128]{2,1,0:T(8,128)} %get-tuple-element.202, s32[64]{0:T(128)S(1)} %compare_select_fusion.7, f32[64,128,128]{2,1,0:T(8,128)} %fusion.21), kind=kCustom, calls=%fused_computation.2.clone.1 | custom fusion | flops 1048576 | bytes 12583168 | tf_op jit(solution)/shard_map/while/body/eval_jaxpr/scatter-add | solution.py:33
  137.9 4.2 fusion.21
  142.9 13.8 %scatter_fusion = f32[128,128,128]{2,1,0:T(8,128)} fusion(f32[128,128,128]{2,1,0:T(8,128)} %get-tuple-element.202, s32[64]{0:T(128)S(1)} %compare_select_fusion.7, f32[64,128,128]{2,1,0:T(8,128)} %fusion.21), kind=kCustom, calls=%fused_computation.2.clone.1 | custom fusion | flops 1048576 | bytes 12583168 | tf_op jit(solution)/shard_map/while/body/eval_jaxpr/scatter-add | solution.py:33
  156.7 4.3 broadcast_in_dim.31
  160.9 27.5 %scatter_fusion.1 = f32[32,4,128,128]{3,2,1,0:T(8,128)} fusion(f32[32,4,128,128]{3,2,1,0:T(8,128)} %broadcast_in_dim.31, s32[128]{0:T(128)S(1)} %fusion.10, f32[128,128,128]{2,1,0:T(8,128)} %get-tuple-element.126), kind=kCustom, calls=%fused_computation.3 | custom fusion | flops 2097152 | bytes 25166848 | tf_op jit(solution)/shard_map/scatter-add | solution.py:46
  188.5 4.6 dynamic-slice_bitcast_fusion
  193.1 4.5 collective-permute-start
  197.6 91.5 %collective-permute-done = f32[16,4,128,128]{3,2,1,0:T(8,128)} collective-permute-done((f32[16,4,128,128]{3,2,1,0:T(8,128)}, f32[16,4,128,128]{3,2,1,0:T(8,128)}, u32[]{:S(2)}, u32[]{:S(2)}) %collective-permute-start) | collective-permute-done | bytes 4194336 | tf_op jit(solution)/shard_map/ppermute | solution.py:10
  289.1 4.2 bitcast_add_fusion
  295.4 3.1 collective-permute-start.1
  298.6 45.4 %collective-permute-done.1 = f32[8,4,128,128]{3,2,1,0:T(8,128)} collective-permute-done((f32[8,4,128,128]{3,2,1,0:T(8,128)S(1)}, f32[8,4,128,128]{3,2,1,0:T(8,128)}, u32[]{:S(2)}, u32[]{:S(2)}) %collective-permute-start.1) | collective-permute-done | bytes 2097184 | tf_op jit(solution)/shard_map/ppermute | solution.py:10
  344.0 2.5 bitcast_add_fusion.1
  347.5 10.9 %collective-permute-start.2 = (f32[4,4,128,128]{3,2,1,0:T(8,128)}, f32[4,4,128,128]{3,2,1,0:T(8,128)}, u32[]{:S(2)}, u32[]{:S(2)}) collective-permute-start(f32[4,4,128,128]{3,2,1,0:T(8,128)} %dynamic-slice_bitcast_fusion.2), channel_id=1, source_target_pairs={{0,64},{16,80},{32,96},{48,112},{64,0},{80,16},{96,32},{112,48},{1... | collective-permute-start | bytes 3145736 | tf_op jit(solution)/shard_map/ppermute | solution.py:10
  358.4 22.1 %collective-permute-done.2 = f32[4,4,128,128]{3,2,1,0:T(8,128)} collective-permute-done((f32[4,4,128,128]{3,2,1,0:T(8,128)}, f32[4,4,128,128]{3,2,1,0:T(8,128)}, u32[]{:S(2)}, u32[]{:S(2)}) %collective-permute-start.2) | collective-permute-done | bytes 1048608 | tf_op jit(solution)/shard_map/ppermute | solution.py:10
  382.8 26.5 %collective-permute-start.3 = (f32[2,4,128,128]{3,2,1,0:T(8,128)S(1)}, f32[2,4,128,128]{3,2,1,0:T(8,128)S(1)}, u32[]{:S(2)}, u32[]{:S(2)}) collective-permute-start(f32[2,4,128,128]{3,2,1,0:T(8,128)S(1)} %dynamic-slice_bitcast_fusion.3), channel_id=1, source_target_pairs={{0,32},{16,48},{32,0},{48,16},{64,96},{80,112},{96,64},{112,80},{1... | collective-permute-start | bytes 1572872 | tf_op jit(solution)/shard_map/ppermute | solution.py:10
  409.3 22.6 %collective-permute-done.3 = f32[2,4,128,128]{3,2,1,0:T(8,128)S(1)} collective-permute-done((f32[2,4,128,128]{3,2,1,0:T(8,128)S(1)}, f32[2,4,128,128]{3,2,1,0:T(8,128)S(1)}, u32[]{:S(2)}, u32[]{:S(2)}) %collective-permute-start.3) | collective-permute-done | bytes 524320 | tf_op jit(solution)/shard_map/ppermute | solution.py:10
  435.0 8.2 %collective-permute-done.4 = f32[1,4,128,128]{3,2,1,0:T(8,128)S(1)} collective-permute-done((f32[1,4,128,128]{3,2,1,0:T(8,128)S(1)}, f32[1,4,128,128]{3,2,1,0:T(8,128)S(1)}, u32[]{:S(2)}, u32[]{:S(2)}) %collective-permute-start.4) | collective-permute-done | bytes 262176 | tf_op jit(solution)/shard_map/ppermute | solution.py:10
  443.9 44.0 %all-gather.3.cloned.1.call-done = bf16[512,2048]{1,0:T(8,128)(2,1)} async-done(((bf16[512,128]{1,0:T(8,128)(2,1)}), bf16[512,2048]{1,0:T(8,128)(2,1)}) %all-gather.3.cloned.1.call-update) | async-done | bytes 2097168 | tf_op jit(solution)/shard_map/all_gather | solution.py:57
  487.9 3.0 fusion.5
  490.9 88.3 %all-gather.5.cloned.1.call-done = bf16[16384,128]{1,0:T(8,128)(2,1)} async-done(((bf16[512,128]{1,0:T(8,128)(2,1)}), bf16[16384,128]{1,0:T(8,128)(2,1)}) %all-gather.5.cloned.1.call-update) | async-done | bytes 4194320 | tf_op jit(solution)/shard_map/all_gather | solution.py:63
  579.2 4.5 fusion.2
  (63 shorter events, 47.4 us)
Async XLA Ops:
  7.2 480.8 %copy-start = (bf16[2048,128]{1,0:T(8,128)(2,1)S(1)}, bf16[2048,128]{1,0:T(8,128)(2,1)}, u32[]{:S(2)}) copy-start(bf16[2048,128]{1,0:T(8,128)(2,1)} %param.16) | copy-start | bytes 1572868
  7.2 480.7 %all-gather.3.cloned.1.call-start = ((), (), s32[]{:S(2)}) async-start(), calls=%async_computation | async-start | bytes 2228224 | tf_op jit(solution)/shard_map/all_gather | solution.py:57
  8.2 4.3 copy-start.1
  193.1 96.0 %collective-permute-start = (f32[16,4,128,128]{3,2,1,0:T(8,128)}, f32[16,4,128,128]{3,2,1,0:T(8,128)}, u32[]{:S(2)}, u32[]{:S(2)}) collective-permute-start(f32[16,4,128,128]{3,2,1,0:T(8,128)} %dynamic-slice_bitcast_fusion), channel_id=1, source_target_pairs={{0,256},{16,272},{32,288},{48,304},{64,320},{80,336},{96,352},{112... | collective-permute-start | bytes 12582920 | tf_op jit(solution)/shard_map/ppermute | solution.py:10
  293.3 2.0 copy-start.2
  295.4 48.5 %collective-permute-start.1 = (f32[8,4,128,128]{3,2,1,0:T(8,128)S(1)}, f32[8,4,128,128]{3,2,1,0:T(8,128)}, u32[]{:S(2)}, u32[]{:S(2)}) collective-permute-start(f32[8,4,128,128]{3,2,1,0:T(8,128)S(1)} %dynamic-slice_bitcast_fusion.1), channel_id=1, source_target_pairs={{0,128},{16,144},{32,160},{48,176},{64,192},{80,208},{96,224},{112... | collective-permute-start | bytes 6291464 | tf_op jit(solution)/shard_map/ppermute | solution.py:10
  347.5 33.0 %collective-permute-start.2 = (f32[4,4,128,128]{3,2,1,0:T(8,128)}, f32[4,4,128,128]{3,2,1,0:T(8,128)}, u32[]{:S(2)}, u32[]{:S(2)}) collective-permute-start(f32[4,4,128,128]{3,2,1,0:T(8,128)} %dynamic-slice_bitcast_fusion.2), channel_id=1, source_target_pairs={{0,64},{16,80},{32,96},{48,112},{64,0},{80,16},{96,32},{112,48},{1... | collective-permute-start | bytes 3145736 | tf_op jit(solution)/shard_map/ppermute | solution.py:10
  381.8 1.0 copy-start.3
  381.8 197.4 %copy-start.4 = (s32[16]{0:T(128)S(1)}, s32[16]{0:T(128)}, u32[]{:S(2)}) copy-start(s32[16]{0:T(128)} %param.17) | copy-start | bytes 196
  382.8 49.1 %collective-permute-start.3 = (f32[2,4,128,128]{3,2,1,0:T(8,128)S(1)}, f32[2,4,128,128]{3,2,1,0:T(8,128)S(1)}, u32[]{:S(2)}, u32[]{:S(2)}) collective-permute-start(f32[2,4,128,128]{3,2,1,0:T(8,128)S(1)} %dynamic-slice_bitcast_fusion.3), channel_id=1, source_target_pairs={{0,32},{16,48},{32,0},{48,16},{64,96},{80,112},{96,64},{112,80},{1... | collective-permute-start | bytes 1572872 | tf_op jit(solution)/shard_map/ppermute | solution.py:10
  433.1 10.1 %collective-permute-start.4 = (f32[1,4,128,128]{3,2,1,0:T(8,128)S(1)}, f32[1,4,128,128]{3,2,1,0:T(8,128)S(1)}, u32[]{:S(2)}, u32[]{:S(2)}) collective-permute-start(f32[1,4,128,128]{3,2,1,0:T(8,128)S(1)} %constant_dynamic-slice_fusion), channel_id=1, source_target_pairs={{0,16},{16,0},{32,48},{48,32},{64,80},{80,64},{96,112},{112,96},{1... | collective-permute-start | bytes 786440 | tf_op jit(solution)/shard_map/ppermute | solution.py:10
  443.9 135.3 %all-gather.5.cloned.1.call-start = ((), (), s32[]{:S(2)}) async-start(), calls=%async_computation.1 | async-start | bytes 4325376 | tf_op jit(solution)/shard_map/all_gather | solution.py:63
Sparse Core Ops, SparseCore 0:
  444.0 43.8 all-gather.2
  491.7 87.4 all-gather.4
where the time goes:
time: 594 us; the launch traced here: 592 us
  waiting for transfers between devices  322 us (54%)
  other arithmetic  129 us (22%)
  starting transfers between devices  47 us (8%)
  local copies, waits for them, and re-layouts  46.2 us (8%)
  matrix products  33 us (6%)
  between operations  14.2 us (2%)
    ppermute x5, waiting for transfers between devices, swapped(): lax.ppermute(x, axis, [(i, i ^ 1 << stride) for i in range(lax.axis_size(...  190 us
    all_gather x1, waiting for transfers between devices, local(): lax.all_gather(hidden, 'edge', axis=0, tiled=True)  88.3 us
    scatter-add x6, other arithmetic, add_group(): return partial_value.at[slots].add(product)  82.4 us
    ppermute x5, starting transfers between devices, swapped(): lax.ppermute(x, axis, [(i, i ^ 1 << stride) for i in range(lax.axis_size(...  46.9 us
    all_gather x1, waiting for transfers between devices, local(): lax.all_gather(aggregated, 'feat', axis=1, tiled=True)  44 us
    scatter-add x1, other arithmetic, local(): dense = jnp.zeros((edge_count, local_blocks, block_size, width), jnp.floa...  27.5 us
    dot_general x6, matrix products, add_group(): jnp.einsum('gij,gjc->gic', tiles[chosen], inputs[columns], preferred_elem...  25.5 us
    gather x6, local copies, waits for them, and re-layouts, add_group(): tiles[chosen]  14.2 us
  transfers between devices with their start and end apart: 7, of which 7 were waited for; matrix products, arithmetic and copies ran while one was open for 0% of the time, Pallas kernels for 0%

commit v1 on v0

v1 whole, which is shorter than its diff:
```python
import functools

import jax
import jax.numpy as jnp
import numpy as np
from jax import lax
from jax.experimental import pallas as pl
from jax.experimental.pallas import tpu as pltpu
from jax.sharding import PartitionSpec as P

NX, NZ, NY, NC = 4, 8, 8, 2
HOP_US = 1.5
LINK = 46.5e3
MESH_ID = pl.DeviceIdType.MESH
SIGNS = (1, -1)


def offsets(n):
    h = n // 2
    out = [h] if n > 1 else []
    for r in range(h - 1, 0, -1):
        out += [r, n - r]
    return out + [0]


def halves_of(sign, r, n):
    lead = 0 if sign > 0 else 1
    return [lead] if r == n // 2 else [1 - lead, lead]


class Plan:
    def __init__(self):
        self.steps = {}
        self.units = {}

    def unit(self, name, link, blocks, src, dst):
        self.units[name] = dict(link=link, blocks=blocks, src=src, dst=dst, index=len(self.units))

    def step(self, name, fn=None, after=(), recv=(), send=(), cost=0.02):
        self.steps[name] = dict(fn=fn, after=list(after), recv=[r for r in recv if r in self.units or True], send=list(send), cost=cost)

    def order(self, block_bytes):
        sender = {u: s for s, v in self.steps.items() for u in v["send"]}
        needed = {s: [] for s in self.steps}
        for s, v in self.steps.items():
            for a in v["after"]:
                needed[a].append((s, 0.0))
            for u in v["recv"]:
                wire = self.units[u]["blocks"] * block_bytes / LINK
                needed[sender[u]].append((s, wire + HOP_US))
        path = {}

        def length(s):
            if s not in path:
                path[s] = self.steps[s]["cost"] + max([d + length(t) for t, d in needed[s]] + [0.0])
            return path[s]

        for s in self.steps:
            length(s)
        core, links, arrival, done, left, result = 0.0, {}, {}, {}, set(self.steps), []
        names = list(self.steps)
        while left:
            best = None
            for s in names:
                v = self.steps[s]
                if s not in left or any(a not in done for a in v["after"]) or any(u not in arrival for u in v["recv"]):
                    continue
                ready = max([done[a] for a in v["after"]] + [arrival[u] for u in v["recv"]] + [core])
                key = (ready, -path[s])
                if best is None or key < best[0]:
                    best = (key, s)
            (ready, _), s = best
            left.remove(s)
            result.append(s)
            core = ready + self.steps[s]["cost"]
            done[s] = core
            for u in self.steps[s]["send"]:
                link = self.units[u]["link"]
                rate = LINK if link[0] != "core" else 8 * LINK
                begin = max(core, links.get(link, 0.0))
                links[link] = begin + self.units[u]["blocks"] * block_bytes / rate
                arrival[u] = links[link] + HOP_US
        self.total = core
        return result


def need_order():
    zu = {s: [(r, half) for r in range(NZ // 2, 0, -1) for half in halves_of(s, r, NZ)] for s in SIGNS}
    subs = 2 if NZ >= 4 else 1
    xu = {s: [] for s in SIGNS}
    for s in SIGNS:
        for r in range(NX // 2, 0, -1):
            for sub in range(subs):
                xu[s] += [(r, half, sub) for half in halves_of(s, r, NX)]
    zoff, xoff = offsets(NZ), offsets(NX)
    width = NZ // subs
    blocks, where, seg = [], {}, []
    slots = max(len(zu[1]), len(xu[1]))
    for t in range(slots):
        begin = len(blocks)
        for s in SIGNS:
            if t < len(zu[s]):
                r, half = zu[s][t]
                where["z", s, r, half] = (len(blocks), t)
                blocks += [(rx, s * r % NZ, half) for rx in xoff]
        for s in SIGNS:
            if t < len(xu[s]):
                r, half, sub = xu[s][t]
                where["x", s, r, half, sub] = (len(blocks), t)
                blocks += [(s * r % NX, rz, 2 + half) for rz in zoff[sub * width:(sub + 1) * width]]
        seg.append((begin, len(blocks)))
    begin = len(blocks)
    for sub in range(subs):
        for half in (0, 1):
            where["x", 0, half, sub] = (len(blocks), slots)
            blocks += [(0, rz, 2 + half) for rz in zoff[sub * width:(sub + 1) * width]]
    for half in (0, 1):
        where["z", 0, half] = (len(blocks), slots)
        blocks += [(rx, 0, half) for rx in xoff]
    seg.append((begin, len(blocks)))
    return zu, xu, subs, blocks, where, seg


def kernel(plan_only, table, picks, features, tiles, weight, hidden, ghosts, *scratch):
    (bank, mix, part, zs, zr, xs, xr, z2s, z2r, x2s, x2r, qz, qx, gy, g, send_sem, recv_sem, local_sem) = scratch
    zu, xu, subs, blocks, where, seg = need_order()
    plan = Plan()
    hx, hz, hy = NX // 2, NZ // 2, NY // 2
    zoff, xoff = offsets(NZ), offsets(NX)
    width = NZ // subs
    size = features.shape[1]
    rows = features.shape[0] // 4
    deep = tiles.shape[0]
    if not plan_only:
        edge, feat = lax.axis_index("edge"), lax.axis_index("feat")
        x, z, y, core = edge // NZ, edge % NZ, feat // NC, feat % NC
        peers = {}
        for s in SIGNS:
            peers["x", s] = (((x + s + NX) % NX) * NZ + z, feat)
            peers["z", s] = (x * NZ + (z + s + NZ) % NZ, feat)
            peers["y", s] = (edge, ((y + s + NY) % NY) * NC + core)
        peers["core", 1] = (edge, y * NC + (core + 1) % NC)
        greeted = [k for k, n in ((("x", 1), NX), (("x", -1), NX), (("z", 1), NZ), (("z", -1), NZ), (("y", 1), NY), (("y", -1), NY), (("core", 1), NC)) if n > 1]
        loads = [pltpu.make_async_copy(tiles, bank.at[pl.ds(0, deep)], local_sem.at[0])]
        for ry in range(NY):
            for rc in range(NC):
                row = ((y + ry) % NY * NC + (core + rc) % NC) * size
                loads.append(
                    pltpu.make_async_copy(
                        weight.at[pl.ds(pl.multiple_of(row, size), size)],
                        mix.at[pl.ds((ry * NC + rc) * size, size)],
                        local_sem.at[1 + ry * NC + rc],
                    )
                )
        for c in loads:
            c.start()
        barrier = pltpu.get_barrier_semaphore()
        for k in greeted:
            pl.semaphore_signal(barrier, inc=1, device_id=peers[k], device_id_type=MESH_ID)
        bank[deep] = jnp.zeros_like(bank[deep])
        loads[0].wait()

    def products(lo, hi):
        def body(i, carry):
            wide = jnp.concatenate([bank[table[i * 4 + c]] for c in range(4)], axis=1)
            part[i] = jnp.dot(wide, features[...], preferred_element_type=jnp.float32)
            return carry

        lax.fori_loop(lo, hi, body, 0)

    def total(count, own, extra, put):
        def body(k, carry):
            value = own(k)
            for e in extra:
                value = value + e(k).astype(jnp.float32)
            put(k, value)
            return carry

        lax.fori_loop(0, count, body, 0) if count > 1 else body(0, 0)

    for t, (lo, hi) in enumerate(seg):
        plan.step(("P", t), functools.partial(products, lo, hi), cost=0.05 * (hi - lo), after=[("P", t - 1)] if t else [])

    def exists(sign, r, half, n):
        return 1 <= r <= n // 2 and half in halves_of(sign, r, n)

    def store(ref, *lead):
        def put(k, value):
            ref[(*lead, k)] = value.astype(ref.dtype)

        return put

    def put_one(ref, *lead):
        def put(k, value):
            ref[lead] = value.astype(ref.dtype)

        return put

    zi = {s: {u: i for i, u in enumerate(zu[s])} for s in SIGNS}
    for s in SIGNS:
        d = 0 if s > 0 else 1
        for (r, half), i in zi[s].items():
            plan.unit(("Z1", s, r, half), ("z", s), NX, (zs, (d, i)), (zr, (d, i)))
    for s in SIGNS:
        d = 0 if s > 0 else 1
        for (r, half), i in zi[s].items():
            base, t = where["z", s, r, half]
            back = exists(s, r + 1, half, NZ)
            extra = [functools.partial(lambda d, j, k: zr[d, j, k], d, zi[s][r + 1, half])] if back else []
            plan.step(
                ("Z1", s, r, half),
                functools.partial(total, NX, functools.partial(lambda b, k: part[b + k], base), extra, store(zs, d, i)),
                after=[("P", t)], recv=[("Z1", s, r + 1, half)] if back else [], send=[("Z1", s, r, half)], cost=0.15,
            )
    for half in (0, 1):
        base, t = where["z", 0, half]
        near = [s for s in SIGNS if exists(s, 1, half, NZ)]
        plan.step(
            ("Z1f", half),
            functools.partial(total, NX, functools.partial(lambda b, k: part[b + k], base),
                              [functools.partial(lambda d, j, k: zr[d, j, k], 0 if s > 0 else 1, zi[s][1, half]) for s in near], store(qz, half)),
            after=[("P", t)], recv=[("Z1", s, 1, half) for s in near], cost=0.15,
        )

    xi = {s: {u: i for i, u in enumerate(xu[s])} for s in SIGNS}
    for s in SIGNS:
        d = 0 if s > 0 else 1
        for (r, half, sub), i in xi[s].items():
            plan.unit(("X1", s, r, half, sub), ("x", s), width, (xs, (d, i)), (xr, (d, i)))
    for s in SIGNS:
        d = 0 if s > 0 else 1
        for (r, half, sub), i in xi[s].items():
            base, t = where["x", s, r, half, sub]
            back = exists(s, r + 1, half, NX)
            extra = [functools.partial(lambda d, j, k: xr[d, j, k], d, xi[s][r + 1, half, sub])] if back else []
            plan.step(
                ("X1", s, r, half, sub),
                functools.partial(total, width, functools.partial(lambda b, k: part[b + k], base), extra, store(xs, d, i)),
                after=[("P", t)], recv=[("X1", s, r + 1, half, sub)] if back else [], send=[("X1", s, r, half, sub)], cost=0.15,
            )
    for sub in range(subs):
        for half in (0, 1):
            base, t = where["x", 0, half, sub]
            near = [s for s in SIGNS if exists(s, 1, half, NX)]

            def put(k, value, half=half, sub=sub):
                qx[half, sub * width + k] = value

            plan.step(
                ("X1f", half, sub),
                functools.partial(total, width, functools.partial(lambda b, k: part[b + k], base),
                                  [functools.partial(lambda d, j, k: xr[d, j, k], 0 if s > 0 else 1, xi[s][1, half, sub]) for s in near], put),
                after=[("P", t)], recv=[("X1", s, 1, half, sub) for s in near], cost=0.15,
            )

    for tag, axis, n, off, q, sref, rref, first in (
        ("Z2", "x", NX, xoff, qz, z2s, z2r, lambda half, p: [("Z1f", half)]),
        ("X2", "z", NZ, zoff, qx, x2s, x2r, lambda half, p: [("X1f", half, p // width)]),
    ):
        units = {s: [(r, half) for r in range(n // 2, 0, -1) for half in halves_of(s, r, n)] for s in SIGNS}
        for s in SIGNS:
            d = 0 if s > 0 else 1
            for i, (r, half) in enumerate(units[s]):
                plan.unit((tag, s, r, half), (axis, s), 1, (sref, (d, i)), (rref, (d, i)))
        for s in SIGNS:
            d = 0 if s > 0 else 1
            for i, (r, half) in enumerate(units[s]):
                p = off.index(s * r % n)
                back = exists(s, r + 1, half, n)
                extra = []
                if back:
                    extra = [functools.partial(lambda ref, d, j, k: ref[d, j], rref, d, units[s].index((r + 1, half)))]
                plan.step(
                    (tag, s, r, half),
                    functools.partial(total, 1, functools.partial(lambda q, half, p, k: q[half, p], q, half, p), extra, put_one(sref, d, i)),
                    after=first(half, p), recv=[(tag, s, r + 1, half)] if back else [], send=[(tag, s, r, half)], cost=0.05,
                )
        for half in (0, 1):
            near = [s for s in SIGNS if exists(s, 1, half, n)]
            p = off.index(0)
            plan.step(
                (tag + "f", half),
                functools.partial(total, 1, functools.partial(lambda q, half, p, k: q[half, p], q, half, p),
                                  [functools.partial(lambda ref, d, j, k: ref[d, j], rref, 0 if s > 0 else 1, units[s].index((1, half))) for s in near],
                                  put_one(gy, 0 if tag == "Z2" else 1, 0, 0, half)),
                after=first(half, p), recv=[(tag, s, 1, half) for s in near], cost=0.05,
            )

    for f in (0, 1):
        ready = [(("Z2f", "X2f")[f], half) for half in (0, 1)]
        arrivals = []

        def part_of(sign, d, n):
            if d + 1 < n // 2:
                return 0, 2
            return (0 if sign > 0 else 1), 1

        if NC > 1:
            plan.unit(("YP", f, 0), ("core", 1), 2, (gy, (f, 0, 0)), (gy, (f, 0, 1)))
            arrivals.append(("YP", f, 0))
        for s in SIGNS:
            for d in range(hy):
                a, c = part_of(s, d, NY)
                here, there = -s * d % NY, -s * (d + 1) % NY
                plan.unit(("Y", f, s, d), ("y", s), c, (gy, (f, here, 0, pl.ds(a, c))), (gy, (f, there, 0, pl.ds(a, c))))
                arrivals.append(("Y", f, s, d))
                if NC > 1:
                    plan.unit(("YP", f, s, d + 1), ("core", 1), c, (gy, (f, there, 0, pl.ds(a, c))), (gy, (f, there, 1, pl.ds(a, c))))
                    arrivals.append(("YP", f, s, d + 1))
        send = ([("Y", f, s, 0) for s in SIGNS] if NY > 1 else []) + ([("YP", f, 0)] if NC > 1 else [])
        plan.step(("Yown", f), after=ready, send=send)
        for s in SIGNS:
            for d in range(1, hy + 1):
                send = ([("Y", f, s, d)] if d < hy else []) + ([("YP", f, s, d)] if NC > 1 else [])
                plan.step(("Yfwd", f, s, d), recv=[("Y", f, s, d - 1)], send=send)

        def mixing(f=f):
            for half in (0, 1):
                wide = jnp.concatenate([gy[f, ry, rc, half] for ry in range(NY) for rc in range(NC)], axis=1)
                value = jnp.maximum(jnp.dot(wide, mix[...], preferred_element_type=jnp.float32), 0.0).astype(jnp.bfloat16)
                g[f * NX * NZ * 2 + half] = value
                hidden[pl.ds((2 * f + half) * rows, rows)] = value

        plan.step(("H", f), mixing, after=[("W",), ("Yown", f)], recv=arrivals, cost=1.0)

    def weights():
        for c in loads[1:]:
            c.wait()

    plan.step(("W",), weights, after=[("P", len(seg) - 1)])

    everything = []
    for f in (0, 1):
        (a1, n1), (a2, n2) = ((("x", NX), ("z", NZ)), (("z", NZ), ("x", NX)))[f]

        def slot(q1, q2, a=0, f=f, n2=n2):
            return f * NX * NZ * 2 + (q1 * n2 + q2) * 2 + a

        def gref(q1, q2, a, c, slot=slot):
            return (g, (pl.ds(slot(q1, q2, a), c),))

        for s in SIGNS:
            for d in range(n1 // 2):
                a, c = part_of(s, d, n1)
                plan.unit(("E1", f, s, d), (a1, s), c, gref(-s * d % n1, 0, a, c), gref(-s * (d + 1) % n1, 0, a, c))
                everything.append(("E1", f, s, d))
        for q in range(n1):
            for s in SIGNS:
                for d in range(n2 // 2):
                    a, c = part_of(s, d, n2)
                    plan.unit(("E2", f, q, s, d), (a2, s), c, gref(q, -s * d % n2, a, c), gref(q, -s * (d + 1) % n2, a, c))
                    everything.append(("E2", f, q, s, d))
        plan.step(("Eown", f), after=[("H", f)], send=[("E1", f, s, 0) for s in SIGNS] + [("E2", f, 0, s, 0) for s in SIGNS])
        for d in range(1, n1 // 2 + 1):
            for s in SIGNS:
                if d < n1 // 2:
                    q = -s * d % n1
                    plan.step(("E1f", f, s, d), recv=[("E1", f, s, d - 1)], send=[("E1", f, s, d)] + [("E2", f, q, t, 0) for t in SIGNS])
            if d == n1 // 2:
                plan.step(("E1f", f, 0, d), recv=[("E1", f, s, d - 1) for s in SIGNS], send=[("E2", f, d, t, 0) for t in SIGNS])
        for q in range(n1):
            for s in SIGNS:
                for d in range(1, n2 // 2):
                    plan.step(("E2f", f, q, s, d), recv=[("E2", f, q, s, d - 1)], send=[("E2", f, q, s, d)])

    def gather():
        def body(r, carry):
            ghosts[pl.ds(pl.multiple_of(r * rows, rows), rows)] = g[picks[r]]
            return carry

        lax.fori_loop(0, picks.shape[0], body, 0)

    plan.step(("G",), gather, after=[("H", 0), ("H", 1)], recv=everything, cost=1.0)

    order = plan.order(rows * size * 2)
    if plan_only:
        return plan, order

    def copy(name):
        u = plan.units[name]
        (sref, sat), (dref, dat) = u["src"], u["dst"]
        return pltpu.make_async_remote_copy(
            src_ref=sref.at[sat], dst_ref=dref.at[dat], send_sem=send_sem.at[u["index"]], recv_sem=recv_sem.at[u["index"]],
            device_id=peers[u["link"]], device_id_type=MESH_ID,
        )

    copies = {name: copy(name) for name in plan.units}
    arrived, opened = set(), False
    for name in order:
        step = plan.steps[name]
        for u in step["recv"]:
            if u not in arrived:
                copies[u].wait_recv()
                arrived.add(u)
        if step["fn"] is not None:
            step["fn"]()
        if step["send"] and not opened:
            pl.semaphore_wait(barrier, len(greeted))
            opened = True
        for u in step["send"]:
            copies[u].start()
    for name in plan.units:
        if name not in arrived:
            copies[name].wait_recv()
        copies[name].wait_send()


def scratch_shapes(rows, size, deep):
    zu, xu, subs, blocks, where, seg = need_order()
    width = NZ // subs
    bf, fp = jnp.bfloat16, jnp.float32

    def units(n):
        return len([1 for r in range(n // 2, 0, -1) for half in halves_of(1, r, n)])

    v = pltpu.VMEM
    shapes = [
        v((deep + 1, rows, rows), bf), v((NY * NC * size, size), bf), v((len(blocks), rows, size), fp),
        v((2, len(zu[1]), NX, rows, size), bf), v((2, len(zu[1]), NX, rows, size), bf),
        v((2, len(xu[1]), width, rows, size), bf), v((2, len(xu[1]), width, rows, size), bf),
        v((2, units(NX), rows, size), bf), v((2, units(NX), rows, size), bf),
        v((2, units(NZ), rows, size), bf), v((2, units(NZ), rows, size), bf),
        v((2, NX, rows, size), fp), v((2, NZ, rows, size), fp),
        v((2, NY, NC, 2, rows, size), bf), v((4 * NX * NZ, rows, size), bf),
    ]
    return shapes


def local(features, tiles, tile_slot, tile_col, tile_id, touched, weight, readers):
    edge = lax.axis_index("edge")
    x, z = edge // NZ, edge % NZ
    block = tiles.shape[1]
    size = features.shape[1]
    deep = tiles.shape[0]
    cap = touched.shape[2]
    zu, xu, subs, blocks, where, seg = need_order()
    at = np.array(blocks, np.int32)
    owner = (x + at[:, 0]) % NX * NZ + (z + at[:, 1]) % NZ
    wanted = owner * 4 + at[:, 2]
    mine = lax.dynamic_index_in_dim(touched, edge, 0, keepdims=False).reshape(-1)
    slots = jnp.arange(mine.shape[0], dtype=jnp.int32)
    target_of = slots // cap * 4 + mine
    target = jnp.sum(jnp.where(tile_slot[:, None] == slots[None, :], target_of[None, :], 0), axis=1)
    pair = target * 4 + tile_col
    keys = (wanted[:, None] * 4 + jnp.arange(4, dtype=jnp.int32)[None, :]).reshape(-1)
    table = deep + jnp.sum(jnp.where(keys[:, None] == pair[None, :], tile_id[None, :] - deep, 0), axis=1)
    o, j = readers // 4, readers % 4
    rx, rz = (o // NZ - x + NX) % NX, (o % NZ - z + NZ) % NZ
    picks = jnp.where(j < 2, (rx * NZ + rz) * 2 + j, NX * NZ * 2 + (rz * NX + rx) * 2 + j - 2)
    plan, order = kernel(True, table, picks, features, tiles, weight, None, None, *([None] * 18))
    count = len(plan.units)
    vmem = pl.BlockSpec(memory_space=pltpu.VMEM)
    smem = pl.BlockSpec(memory_space=pltpu.SMEM)
    anywhere = pl.BlockSpec(memory_space=pl.ANY)
    hidden, ghosts = pl.pallas_call(
        functools.partial(kernel, False),
        out_shape=(
            jax.ShapeDtypeStruct(features.shape, jnp.bfloat16),
            jax.ShapeDtypeStruct((readers.shape[0] * block, size), jnp.bfloat16),
        ),
        in_specs=[smem, smem, vmem, anywhere, anywhere],
        out_specs=(vmem, vmem),
        scratch_shapes=scratch_shapes(block, size, deep)
        + [pltpu.SemaphoreType.DMA((count,)), pltpu.SemaphoreType.DMA((count,)), pltpu.SemaphoreType.DMA((1 + NY * NC,))],
        compiler_params=pltpu.CompilerParams(collective_id=0, has_side_effects=True, vmem_limit_bytes=52 << 20),
        name="layer",
    )(table.astype(jnp.int32), picks.astype(jnp.int32), features, tiles, weight)
    return hidden, ghosts


def solution(mesh):
    in_specs = (
        P("edge", "feat"),
        P("edge", None, None),
        P("edge"),
        P("edge"),
        P("edge"),
        P(),
        P(None, "feat"),
        P("edge"),
    )
    out_specs = (P("edge", "feat"), P("edge", "feat"))
    return jax.shard_map(local, mesh=mesh, in_specs=in_specs, out_specs=out_specs, check_vma=False)
```

time: 594 us -> 118 us (0.20)
  waiting for transfers between devices: 322 us -> 0 us
  other arithmetic: 129 us -> 3.34 us
  Pallas kernels: 0 us -> 110 us
  starting transfers between devices: 47 us -> 0 us
  local copies, waits for them, and re-layouts: 46.2 us -> 3.71 us
  matrix products: 33 us -> 0 us
  between operations: 14.2 us -> 0.72 us
    ppermute x5 -> x0, waiting for transfers between devices: 190 us -> none  [swapped(): lax.ppermute(x, axis, [(i, i ^ 1 << stride) for i in range(lax.axis_size(...]
    all_gather x2 -> x0, waiting for transfers between devices: 132 us -> none  [the longest x1 88.3 us: local(): lax.all_gather(hidden, 'edge', axis=0, tiled=True)]
    pallas_call x0 -> x1, Pallas kernels: none -> 110 us  [local(): pl.pallas_call(functools.partial(kernel, False), out_shape=(jax.ShapeDtyp...]
    scatter-add x7 -> x0, other arithmetic: 110 us -> none  [the longest x6 82.4 us: add_group(): return partial_value.at[slots].add(product)]
    ppermute x5 -> x0, starting transfers between devices: 46.9 us -> none  [swapped(): lax.ppermute(x, axis, [(i, i ^ 1 << stride) for i in range(lax.axis_size(...]
    dot_general x8 -> x0, matrix products: 33 us -> none  [the longest x6 25.5 us: add_group(): jnp.einsum('gij,gjc->gic', tiles[chosen], inputs[columns], preferred_elem...]
    gather x12 -> x0, local copies, waits for them, and re-layouts: 27 us -> none  [the longest x6 14.2 us: add_group(): tiles[chosen]]
    broadcast_in_dim x2 -> x0, local copies, waits for them, and re-layouts: 8.56 us -> none  [the longest x1 4.29 us: local(): jnp.zeros((slot_total, block_size, width), jnp.float32)]
  transfers between devices with their start and end apart: 7 -> 0, of which waited for: 7 -> 0; matrix products, arithmetic and copies ran while one was open for 0% -> 0% of each run, Pallas kernels for 0% -> 0%
where the time goes in v1:
time: 118 us
  Pallas kernels  110 us (93%)
  local copies, waits for them, and re-layouts  3.71 us (3%)
  other arithmetic  3.34 us (3%)
    pallas_call x1, Pallas kernels, local(): pl.pallas_call(functools.partial(kernel, False), out_shape=(jax.ShapeDtyp...  110 us
    unnamed x8, local copies, waits for them, and re-layouts  3.4 us

profile of v1, /device:TPU:8, one launch (start us, length us, event | category | flops | bytes accessed | tf_op | source)
XLA Modules:
  0.0 117.7 jit_solution(17756534938505414114)
XLA Ops:
  0.6 0.0 copy-start
  0.7 0.7 fusion.6
  1.4 0.7 compare_select_fusion.8.picks
  2.1 0.0 copy-done
  2.1 0.1 copy.15
  2.2 0.1 reshape.47
  2.3 0.9 select_reduce_fusion.1
  3.2 0.7 multiply_add_fusion
  3.9 0.1 iota_add_fusion
  4.0 0.1 add.134
  4.1 0.2 select_reduce_fusion
  4.4 0.0 copy-start.1
  4.4 1.0 copy-done.1
  5.4 0.0 copy-start.2
  5.4 0.9 copy-done.2
  6.3 109.9 %layer.1 = (bf16[512,128]{1,0:T(8,128)(2,1)S(1)}, bf16[2048,128]{1,0:T(8,128)(2,1)S(1)}) custom-call(s32[512]{0:T(512)S(1)} %broadcast_add_fusion.table, s32[16]{0:T(128)S(1)} %compare_select_fusion.8.picks, bf16[512,128]{1,0:T(8,128)(2,1)S(1)} %copy-done.2, bf16[48,128,128]{2,1,0:T(8,128)(2,1)} %tiles.1, bf16[2048,128]{1,0:T(8,128)(2,1)S(1)} %copy-done.1), custom_call_target="tpu_custom_call" | custom-call | tf_op jit(solution)/shard_map/layer/pallas_call | solution.py:455
  116.2 0.7 copy.18
  116.9 0.8 copy.19
  (3 shorter events, 0.0 us)
Async XLA Ops:
  0.6 1.4 %copy-start = (s32[32,32,4]{1,2,0:T(4,128)S(1)}, s32[32,32,4]{1,2,0:T(4,128)}, u32[]{:S(2)}) copy-start(s32[32,32,4]{1,2,0:T(4,128)} %param.16) | copy-start | bytes 49156
  4.4 1.0 copy-start.1
  5.4 0.9 copy-start.2

commit v2 on v0

v2 whole, which is shorter than its diff:
```python
import functools

import jax
import jax.numpy as jnp
import numpy as np
from jax import lax
from jax.experimental import pallas as pl
from jax.experimental.pallas import tpu as pltpu
from jax.sharding import PartitionSpec as P

NX, NZ, NY, NC = 4, 8, 8, 2
STREAMS = ("z", "x", "z", "x")
HOP_US, LINK, GROUP_US, AHEAD_US = 1.9, 46.5e3, 0.3, 1.5
MESH_ID = pl.DeviceIdType.MESH
SIGNS = (1, -1)


def offsets(n):
    h = n // 2
    out = [h] if n > 1 else []
    for r in range(h - 1, 0, -1):
        out += [r, n - r]
    return out + [0]


def groups_of(n):
    h = n // 2
    out, at = [[0]], 1
    for d in range(1, h + 1):
        count = 1 if 2 * d == n else 2
        out.append(list(range(at, at + count)))
        at += count
    return out


def lead(sign):
    return 0 if sign > 0 else 1


def halves_of(sign, r, n):
    if not 1 <= r <= n // 2:
        return []
    return [lead(sign)] if r == n // 2 else [0, 1]


def sizes(kind):
    return (NZ, NX) if kind == "z" else (NX, NZ)


def subs_of(kind):
    second = sizes(kind)[1]
    return second // 4 if second > 4 else 1


class Plan:
    def __init__(self):
        self.steps = {}
        self.units = {}

    def unit(self, name, link, blocks, src, dst):
        self.units[name] = dict(link=link, blocks=blocks, src=src, dst=dst, index=len(self.units))

    def step(self, name, fn=None, after=(), recv=(), send=(), cost=0.02, wave=0):
        self.steps[name] = dict(fn=fn, after=list(after), recv=list(recv), send=list(send), cost=cost, wave=wave)

    def order(self, block_bytes):
        sender = {u: s for s, v in self.steps.items() for u in v["send"]}
        needed = {s: [] for s in self.steps}
        for s, v in self.steps.items():
            for a in v["after"]:
                needed[a].append((s, 0.0))
            for u in v["recv"]:
                needed[sender[u]].append((s, self.units[u]["blocks"] * block_bytes / LINK + HOP_US))
        path = {}

        def length(s):
            if s not in path:
                path[s] = self.steps[s]["cost"] + max([d + length(t) for t, d in needed[s]] + [0.0])
            return path[s]

        for s in self.steps:
            length(s)
        core, links, arrival, done, left, result = 0.0, {}, {}, {}, list(self.steps), []
        while left:
            best = None
            for s in left:
                v = self.steps[s]
                if any(a not in done for a in v["after"]) or any(u not in arrival for u in v["recv"]):
                    continue
                ready = max([done[a] for a in v["after"]] + [arrival[u] for u in v["recv"]] + [core])
                begin = max([ready] + [links.get(self.units[u]["link"], 0.0) - AHEAD_US for u in v["send"]])
                key = (round(begin / 0.2), v["wave"], -path[s])
                if best is None or key < best[0]:
                    best = (key, s, ready)
            _, s, ready = best
            left.remove(s)
            result.append(s)
            core = ready + self.steps[s]["cost"]
            done[s] = core
            for u in self.steps[s]["send"]:
                link = self.units[u]["link"]
                rate = LINK if link[0] != "core" else 8 * LINK
                begin = max(core, links.get(link, 0.0))
                links[link] = begin + self.units[u]["blocks"] * block_bytes / rate
                arrival[u] = links[link] + HOP_US
        self.total = core
        return result


def need_order():
    blocks, where, seg = [], {}, []
    for wave in range(len(STREAMS) // 2):
        pair = [2 * wave, 2 * wave + 1]
        rest = {st: [(off, sub) for off in offsets(sizes(STREAMS[st])[0]) for sub in range(subs_of(STREAMS[st]))] for st in pair}
        if NX > 1:
            for st in pair:
                n = sizes(STREAMS[st])[0]
                rank = {o: min(o, n - o) for o in range(n)}
                rest[st].sort(key=lambda u: (u[0] == 0, (rank[u[0]] != n // 2) * u[1], -rank[u[0]]))
        slots = 5
        for t in range(slots):
            begin = len(blocks)
            for st in pair:
                n, second = sizes(STREAMS[st])
                mine = rest[st]
                take = -(-len(mine) // (slots - t))
                for off, sub in mine[:take]:
                    where[st, off, sub] = (len(blocks), len(seg))
                    far = offsets(second)
                    width = second // subs_of(STREAMS[st])
                    for other in far[sub * width:(sub + 1) * width]:
                        blocks.append(((other, off) if STREAMS[st] == "z" else (off, other)) + (st,))
                rest[st] = mine[take:]
            seg.append((wave, begin, len(blocks)))
    return blocks, where, seg


def kernel(plan_only, group, table, lists, readers, seq, features, tiles, weight, hidden, ghosts, *scratch):
    feats, bank, mix, part, gy, g, send_sem, recv_sem, local_sem = scratch[:9]
    per = [scratch[9 + 5 * st:14 + 5 * st] for st in range(len(STREAMS))]
    blocks, where, seg = need_order()
    plan = Plan()
    size = features.shape[1]
    rows = features.shape[0] // 4
    deep = tiles.shape[0]
    mid = rows // 2
    if not plan_only:
        edge, feat = lax.axis_index("edge"), lax.axis_index("feat")
        x, z, y, core = edge // NZ, edge % NZ, feat // NC, feat % NC
        peers = {}
        for s in SIGNS:
            peers["x", s] = (((x + s + NX) % NX) * NZ + z, feat)
            peers["z", s] = (x * NZ + (z + s + NZ) % NZ, feat)
            peers["y", s] = (edge, ((y + s + NY) % NY) * NC + core)
        peers["core", 1] = (edge, y * NC + (core + 1) % NC)
        greeted = [k for k in peers if {"x": NX, "z": NZ, "y": NY, "core": NC}[k[0]] > 1]
        barrier = pltpu.get_barrier_semaphore()
        for k in greeted:
            pl.semaphore_signal(barrier, inc=1, device_id=peers[k], device_id_type=MESH_ID)
        loads = [
            pltpu.make_async_copy(tiles, bank.at[pl.ds(0, deep)], local_sem.at[0]),
            pltpu.make_async_copy(features, feats, local_sem.at[1]),
        ]
        for ry in range(NY):
            row = (y + ry) % NY * NC * size
            loads.append(
                pltpu.make_async_copy(
                    weight.at[pl.ds(pl.multiple_of(row, size), NC * size)],
                    mix.at[pl.ds(ry * NC * size, NC * size)],
                    local_sem.at[2 + ry],
                )
            )
        for c in loads:
            c.start()
        bank[deep] = jnp.zeros_like(bank[deep])
        loads[0].wait()
        loads[1].wait()

    def products(lo, hi):
        def body(i, carry):
            parts = []
            for b in range(group):
                v = seq[i * group + b]
                j = v % 4
                owner = (x + v // 1024) % NX * NZ + (z + v // 4 % 256) % NZ
                slot = jnp.int32(0)
                for c in range(4):
                    slot = slot + jnp.where(lists[owner * 4 + c] == j, c, 0)
                base = (owner * 4 + slot % 4) * 4
                parts.append(jnp.concatenate([bank[table[base + c]] for c in range(4)], axis=1))
            value = jnp.dot(jnp.concatenate(parts, axis=0), feats[...], preferred_element_type=jnp.float32)
            part[pl.ds(i * group, group)] = value.reshape(group, rows, size)
            return carry

        lax.fori_loop(lo // group, hi // group, body, 0)

    for t, (wave, lo, hi) in enumerate(seg):
        plan.step(("P", t), functools.partial(products, lo, hi), cost=GROUP_US * (hi - lo) / 4, after=[("P", t - 1)] if t else [], wave=wave)

    def cut(half):
        return pl.ds(half * mid, mid)

    def total(count, own, extras, put):
        def body(k, carry):
            for half, more in extras:
                value = own(k, half)
                for e in more:
                    value = value + e(k, half).astype(jnp.float32)
                put(k, half, value)
            return carry

        lax.fori_loop(0, count, body, 0) if count > 1 else body(0, 0)

    everything = []
    for st, kind in enumerate(STREAMS):
        wave = st // 2
        n1, n2 = sizes(kind)
        a1, a2 = ("z", "x") if kind == "z" else ("x", "z")
        h1, h2, hy = n1 // 2, n2 // 2, NY // 2
        subs = subs_of(kind)
        width = n2 // subs
        off2 = offsets(n2)
        s1, r1, s2, r2, q = per[st]

        def unit1(s, r, sub, ref, st=st, width=width, n1=n1):
            hv = halves_of(s, r, n1)
            return ref, (lead(s), r - 1, pl.ds(sub * width, width), pl.ds(hv[0] * mid, mid * len(hv)))

        for s in SIGNS:
            for r in range(1, h1 + 1):
                for sub in range(subs):
                    plan.unit(("A", st, s, r, sub), (a1, s), width * len(halves_of(s, r, n1)) / 2, unit1(s, r, sub, s1), unit1(s, r, sub, r1))

        def in1(s, r, sub, k, half, r1=r1, width=width):
            return r1[lead(s), r - 1, sub * width + k, cut(half)]

        for s in SIGNS:
            for r in range(h1, 0, -1):
                for sub in range(subs):
                    base, t = where[st, s * r % n1, sub]

                    def own(k, half, base=base):
                        return part[base + k, cut(half)]

                    def put(k, half, value, s=s, r=r, sub=sub, s1=s1, width=width):
                        s1[lead(s), r - 1, sub * width + k, cut(half)] = value.astype(jnp.bfloat16)

                    extras = [
                        (half, [functools.partial(in1, s, r + 1, sub)] if half in halves_of(s, r + 1, n1) else [])
                        for half in halves_of(s, r, n1)
                    ]
                    plan.step(
                        ("A", st, s, r, sub), functools.partial(total, width, own, extras, put), after=[("P", t)],
                        recv=[("A", st, s, r + 1, sub)] if r < h1 else [], send=[("A", st, s, r, sub)], cost=0.15, wave=wave,
                    )
        for sub in range(subs):
            base, t = where[st, 0, sub]

            def own(k, half, base=base):
                return part[base + k, cut(half)]

            def put(k, half, value, sub=sub, q=q, width=width):
                q[sub * width + k, cut(half)] = value

            extras = [(half, [functools.partial(in1, s, 1, sub) for s in SIGNS if half in halves_of(s, 1, n1)]) for half in (0, 1)]
            plan.step(
                ("Af", st, sub), functools.partial(total, width, own, extras, put), after=[("P", t)],
                recv=[("A", st, s, 1, sub) for s in SIGNS] if n1 > 1 else [], cost=0.15, wave=wave,
            )

        def unit2(s, r, ref, n2=n2):
            hv = halves_of(s, r, n2)
            return ref, (lead(s), r - 1, pl.ds(hv[0] * mid, mid * len(hv)))

        for s in SIGNS:
            for r in range(1, h2 + 1):
                plan.unit(("B", st, s, r), (a2, s), len(halves_of(s, r, n2)) / 2, unit2(s, r, s2), unit2(s, r, r2))

        def in2(s, r, k, half, r2=r2):
            return r2[lead(s), r - 1, cut(half)]

        for s in SIGNS:
            for r in range(h2, 0, -1):
                p = off2.index(s * r % n2)

                def own(k, half, p=p, q=q):
                    return q[p, cut(half)]

                def put(k, half, value, s=s, r=r, s2=s2):
                    s2[lead(s), r - 1, cut(half)] = value.astype(jnp.bfloat16)

                extras = [
                    (half, [functools.partial(in2, s, r + 1)] if half in halves_of(s, r + 1, n2) else []) for half in halves_of(s, r, n2)
                ]
                plan.step(
                    ("B", st, s, r), functools.partial(total, 1, own, extras, put), after=[("Af", st, p // width)],
                    recv=[("B", st, s, r + 1)] if r < h2 else [], send=[("B", st, s, r)], cost=0.06, wave=wave,
                )
        p = off2.index(0)

        def own(k, half, p=p, q=q):
            return q[p, cut(half)]

        def put(k, half, value, st=st):
            gy[st, 0, 0, cut(half)] = value.astype(jnp.bfloat16)

        extras = [(half, [functools.partial(in2, s, 1) for s in SIGNS if half in halves_of(s, 1, n2)]) for half in (0, 1)]
        plan.step(
            ("Bf", st), functools.partial(total, 1, own, extras, put), after=[("Af", st, p // width)],
            recv=[("B", st, s, 1) for s in SIGNS] if n2 > 1 else [], cost=0.06, wave=wave,
        )

        def rows_of(s, d, n):
            hv = halves_of(s, d + 1, n)
            return pl.ds(hv[0] * mid, mid * len(hv)), len(hv) / 2

        arrivals = []
        if NC > 1:
            plan.unit(("YP", st, 0, 0), ("core", 1), 1, (gy, (st, 0, 0)), (gy, (st, 0, 1)))
            arrivals.append(("YP", st, 0, 0))
        for s in SIGNS:
            for d in range(hy):
                w, c = rows_of(s, d, NY)
                here, there = -s * d % NY, -s * (d + 1) % NY
                plan.unit(("Y", st, s, d), ("y", s), c, (gy, (st, here, 0, w)), (gy, (st, there, 0, w)))
                arrivals.append(("Y", st, s, d))
                if NC > 1:
                    plan.unit(("YP", st, s, d + 1), ("core", 1), c, (gy, (st, there, 0, w)), (gy, (st, there, 1, w)))
                    arrivals.append(("YP", st, s, d + 1))
        send = ([("Y", st, s, 0) for s in SIGNS] if NY > 1 else []) + ([("YP", st, 0, 0)] if NC > 1 else [])
        plan.step(("Y", st), after=[("Bf", st)], send=send, wave=wave)
        for s in SIGNS:
            for d in range(1, hy + 1):
                send = ([("Y", st, s, d)] if d < hy else []) + ([("YP", st, s, d)] if NC > 1 else [])
                plan.step(("Y", st, s, d), recv=[("Y", st, s, d - 1)], send=send, wave=wave)

        def slot(qpos, q2, st=st, n1=n1):
            return st * NX * NZ + q2 * n1 + qpos

        def mixing(st=st, slot=slot):
            def wide(swap):
                order = [(ry, (rc + swap) % NC) for ry in range(NY) for rc in range(NC)]
                value = jnp.dot(
                    jnp.concatenate([gy[st, ry, rc] for ry, rc in order], axis=1), mix[...], preferred_element_type=jnp.float32
                )
                value = jnp.maximum(value, 0.0).astype(jnp.bfloat16)
                g[slot(0, 0)] = value
                hidden[pl.ds(st * rows, rows)] = value

            for c in range(NC):
                pl.when(core == c)(functools.partial(wide, c))

        plan.step(("H", st), mixing, after=[("W",), ("Y", st)], recv=arrivals, cost=0.7, wave=wave)

        back1 = offsets(n1)[::-1]
        where1 = {o: i for i, o in enumerate(back1)}
        sets = groups_of(n1)
        for s in SIGNS:
            for d in range(h1):
                w, c = rows_of(s, d, n1)
                plan.unit(
                    ("C", st, s, d), (a1, s), c, (g, (slot(where1[-s * d % n1], 0), w)), (g, (slot(where1[-s * (d + 1) % n1], 0), w))
                )
                everything.append(("C", st, s, d))
        for i, members in enumerate(sets):
            for s in SIGNS:
                for d in range(h2):
                    w, c = rows_of(s, d, n2)
                    here = pl.ds(slot(members[0], -s * d % n2), len(members))
                    there = pl.ds(slot(members[0], -s * (d + 1) % n2), len(members))
                    plan.unit(("D", st, i, s, d), (a2, s), c * len(members), (g, (here, w)), (g, (there, w)))
                    everything.append(("D", st, i, s, d))
        second = lambda i: [("D", st, i, s, 0) for s in SIGNS] if h2 else []
        plan.step(("C", st), after=[("H", st)], send=[("C", st, s, 0) for s in SIGNS] if h1 else [], wave=wave)
        plan.step(("D", st, 0), after=[("H", st)], send=second(0), wave=wave)
        for d in range(1, h1 + 1):
            for s in SIGNS:
                if d < h1:
                    plan.step(("C", st, s, d), recv=[("C", st, s, d - 1)], send=[("C", st, s, d)], wave=wave)
            plan.step(("D", st, d), recv=[("C", st, s, d - 1) for s in SIGNS], send=second(d), wave=wave)
        for i in range(len(sets)):
            for s in SIGNS:
                for d in range(1, h2):
                    plan.step(("D", st, i, s, d), recv=[("D", st, i, s, d - 1)], send=[("D", st, i, s, d)], wave=wave)

    def weights():
        for c in loads[2:]:
            c.wait()

    plan.step(("W",), weights, after=[("P", len(seg) - 1)])

    def place(q, n):
        return jnp.where(2 * q < n, 2 * q, 2 * (n - q) - 1) % n

    def gather():
        def body(r, carry):
            v = readers[r]
            o, j = v // 4, v % 4
            rx, rz = (o // NZ - x + NX) % NX, (o % NZ - z + NZ) % NZ
            at = j * NX * NZ + jnp.where(j % 2 == 0, rx * NZ + place(rz, NZ), rz * NX + place(rx, NX))
            ghosts[pl.ds(pl.multiple_of(r * rows, rows), rows)] = g[at]
            return carry

        lax.fori_loop(0, readers.shape[0], body, 0)

    plan.step(("G",), gather, after=[("H", st) for st in range(len(STREAMS))], recv=everything, cost=0.5, wave=9)

    order = plan.order(rows * size * 2)
    if plan_only:
        return plan, order

    def copy(name):
        u = plan.units[name]
        (sref, sat), (dref, dat) = u["src"], u["dst"]
        return pltpu.make_async_remote_copy(
            src_ref=sref.at[sat], dst_ref=dref.at[dat], send_sem=send_sem.at[u["index"]], recv_sem=recv_sem.at[u["index"]],
            device_id=peers[u["link"]], device_id_type=MESH_ID,
        )

    copies = {name: copy(name) for name in plan.units}
    arrived, opened = set(), False
    for name in order:
        step = plan.steps[name]
        for u in step["recv"]:
            if u not in arrived:
                copies[u].wait_recv()
                arrived.add(u)
        if step["fn"] is not None:
            step["fn"]()
        if step["send"] and not opened:
            pl.semaphore_wait(barrier, len(greeted))
            opened = True
        for u in step["send"]:
            copies[u].start()
    for name in plan.units:
        if name not in arrived:
            copies[name].wait_recv()
        copies[name].wait_send()


def scratch_shapes(rows, size, deep, count):
    bf, fp, v = jnp.bfloat16, jnp.float32, pltpu.VMEM
    blocks, where, seg = need_order()
    shapes = [
        v((4 * rows, size), bf), v((deep + 1, rows, rows), bf), v((NY * NC * size, size), bf), v((len(blocks), rows, size), fp),
        v((len(STREAMS), NY, NC, rows, size), bf), v((len(STREAMS) * NX * NZ, rows, size), bf),
        pltpu.SemaphoreType.DMA((count,)), pltpu.SemaphoreType.DMA((count,)), pltpu.SemaphoreType.DMA((2 + NY,)),
    ]
    for kind in STREAMS:
        n1, n2 = sizes(kind)
        first, second = v((2, max(n1 // 2, 1), n2, rows, size), bf), v((2, max(n2 // 2, 1), rows, size), bf)
        shapes += [first, first, second, second, v((n2, rows, size), fp)]
    return shapes


def local(features, tiles, tile_slot, tile_col, tile_id, touched, weight, readers):
    edge = lax.axis_index("edge")
    block = tiles.shape[1]
    size = features.shape[1]
    deep = tiles.shape[0]
    blocks, where, seg = need_order()
    group = 4 if all((hi - lo) % 4 == 0 for _, lo, hi in seg) else 1
    seq = jnp.array([rx * 1024 + rz * 4 + j for rx, rz, j in blocks], jnp.int32)
    lists = lax.dynamic_index_in_dim(touched, edge, 0, keepdims=False).reshape(-1)
    keys = jnp.arange(lists.shape[0] * 4, dtype=jnp.int32)
    pair = tile_slot * 4 + tile_col
    table = deep + jnp.sum(jnp.where(keys[:, None] == pair[None, :], tile_id[None, :] - deep, 0), axis=1)
    args = (table.astype(jnp.int32), lists, readers, seq, features, tiles, weight)
    plan, order = kernel(True, group, *args, None, None, *([None] * 29))
    vmem = pl.BlockSpec(memory_space=pltpu.VMEM)
    smem = pl.BlockSpec(memory_space=pltpu.SMEM)
    hbm = pl.BlockSpec(memory_space=pltpu.HBM)
    return pl.pallas_call(
        functools.partial(kernel, False, group),
        out_shape=(
            jax.ShapeDtypeStruct(features.shape, jnp.bfloat16),
            jax.ShapeDtypeStruct((readers.shape[0] * block, size), jnp.bfloat16),
        ),
        in_specs=[smem, smem, smem, smem, hbm, hbm, hbm],
        out_specs=(vmem, vmem),
        scratch_shapes=scratch_shapes(block, size, deep, len(plan.units)),
        compiler_params=pltpu.CompilerParams(collective_id=0, has_side_effects=True, vmem_limit_bytes=60 << 20),
        name="layer",
    )(*args)


def solution(mesh):
    in_specs = (
        P("edge", "feat"),
        P("edge", None, None),
        P("edge"),
        P("edge"),
        P("edge"),
        P(),
        P(None, "feat"),
        P("edge"),
    )
    out_specs = (P("edge", "feat"), P("edge", "feat"))
    return jax.shard_map(local, mesh=mesh, in_specs=in_specs, out_specs=out_specs, check_vma=False)
```

time: 594 us -> 107 us (0.18)
  waiting for transfers between devices: 322 us -> 0 us
  other arithmetic: 129 us -> 1.46 us
  Pallas kernels: 0 us -> 99.8 us
  starting transfers between devices: 47 us -> 0 us
  local copies, waits for them, and re-layouts: 46.2 us -> 4.98 us
  matrix products: 33 us -> 0 us
  between operations: 14.2 us -> 0.65 us
    ppermute x5 -> x0, waiting for transfers between devices: 190 us -> none  [swapped(): lax.ppermute(x, axis, [(i, i ^ 1 << stride) for i in range(lax.axis_size(...]
    all_gather x2 -> x0, waiting for transfers between devices: 132 us -> none  [the longest x1 88.3 us: local(): lax.all_gather(hidden, 'edge', axis=0, tiled=True)]
    scatter-add x7 -> x0, other arithmetic: 110 us -> none  [the longest x6 82.4 us: add_group(): return partial_value.at[slots].add(product)]
    pallas_call x0 -> x1, Pallas kernels: none -> 99.8 us  [local(): pl.pallas_call(functools.partial(kernel, False, group), out_shape=(jax.Sh...]
    ppermute x5 -> x0, starting transfers between devices: 46.9 us -> none  [swapped(): lax.ppermute(x, axis, [(i, i ^ 1 << stride) for i in range(lax.axis_size(...]
    dot_general x8 -> x0, matrix products: 33 us -> none  [the longest x6 25.5 us: add_group(): jnp.einsum('gij,gjc->gic', tiles[chosen], inputs[columns], preferred_elem...]
    gather x12 -> x0, local copies, waits for them, and re-layouts: 27 us -> none  [the longest x6 14.2 us: add_group(): tiles[chosen]]
    select_n x12 -> x0, other arithmetic: 9.2 us -> none  [the longest x6 4.66 us: add_group(): inputs[columns]]
  transfers between devices with their start and end apart: 7 -> 0, of which waited for: 7 -> 0; matrix products, arithmetic and copies ran while one was open for 0% -> 0% of each run, Pallas kernels for 0% -> 0%
where the time goes in v2:
time: 107 us
  Pallas kernels  99.8 us (93%)
  local copies, waits for them, and re-layouts  4.98 us (5%)
  other arithmetic  1.46 us (1%)
    pallas_call x1, Pallas kernels, local(): pl.pallas_call(functools.partial(kernel, False, group), out_shape=(jax.Sh...  99.8 us
    unnamed x4, local copies, waits for them, and re-layouts  4.27 us

profile of v2, /device:TPU:8, one launch (start us, length us, event | category | flops | bytes accessed | tf_op | source)
XLA Modules:
  0.0 106.8 jit_solution(17223477151788277388)
XLA Ops:
  0.6 0.0 copy-start
  0.6 0.8 copy-done
  1.5 0.7 multiply_add_fusion
  2.2 0.2 select_reduce_fusion
  2.4 0.6 broadcast_add_fusion.table
  2.9 0.1 copy.13
  3.0 0.6 reshape.11.lists
  3.6 99.8 %layer.1 = (bf16[512,128]{1,0:T(8,128)(2,1)}, bf16[2048,128]{1,0:T(8,128)(2,1)}) custom-call(s32[512]{0:T(512)} %broadcast_add_fusion.table, s32[128]{0:T(128)} %reshape.11.lists, s32[16]{0:T(128)} %readers.1, s32[128]{0:T(128)} %constant.22.clone.seq, bf16[512,128]{1,0:T(8,128)(2,1)} %features.1, bf16[48,128,128]{2,1,0:T(8,128)(2,1)} %tiles.1, ...), custom_call_target="tpu_custom_call" | custom-call | tf_op jit(solution)/shard_map/layer/pallas_call | solution.py:473
  103.4 1.6 %copy.16 = bf16[512,128]{1,0:T(8,128)(2,1)} copy(bf16[512,128]{1,0:T(8,128)(2,1)} %get-tuple-element.6) | data formatting | bytes 262144
  105.0 1.9 %copy.17 = bf16[2048,128]{1,0:T(8,128)(2,1)} copy(bf16[2048,128]{1,0:T(8,128)(2,1)} %get-tuple-element.7) | data formatting | bytes 1048576
  (1 shorter events, 0.0 us)
Async XLA Ops:
  0.6 0.8 copy-start

commit v3 on v2

--- a/solution.py
+++ b/solution.py
@@ -9,8 +9,14 @@
 from jax.sharding import PartitionSpec as P
 
 NX, NZ, NY, NC = 4, 8, 8, 2
-STREAMS = ("z", "x", "z", "x")
-HOP_US, LINK, GROUP_US, AHEAD_US = 1.9, 46.5e3, 0.3, 1.5
+STREAMS = ("x", "z", "x", "z")
+PRE = (False, False, True, True)
+WAVES = (0, 0, 1, 1)
+FIRST = ('z', 'x', 'z', 'x')
+DIRECT = {"B": (), "C": (), "Y": False}
+SUBS = {"z": 2, "x": 4}
+HOP_US, LINK, GROUP_US, AHEAD_US, FAR_US = 2.3, 46.5e3, 0.3, 0.5, 0.8
+LATER_US = (1.5, 0.0)
 MESH_ID = pl.DeviceIdType.MESH
 SIGNS = (1, -1)
 
@@ -48,8 +54,7 @@
 
 
 def subs_of(kind):
-    second = sizes(kind)[1]
-    return second // 4 if second > 4 else 1
+    return SUBS[kind] if sizes(kind)[1] >= 4 else 1
 
 
 class Plan:
@@ -58,7 +63,12 @@
         self.units = {}
 
     def unit(self, name, link, blocks, src, dst):
-        self.units[name] = dict(link=link, blocks=blocks, src=src, dst=dst, index=len(self.units))
+        axis, by = link
+        n = {"x": NX, "z": NZ, "y": NY, "core": NC}[axis]
+        by %= n
+        far = min(by, n - by)
+        way = (axis, 1 if 2 * by <= n else -1)
+        self.units[name] = dict(to=(axis, by), link=way, far=far, blocks=blocks, src=src, dst=dst, index=len(self.units))
 
     def step(self, name, fn=None, after=(), recv=(), send=(), cost=0.02, wave=0):
         self.steps[name] = dict(fn=fn, after=list(after), recv=list(recv), send=list(send), cost=cost, wave=wave)
@@ -70,7 +80,8 @@
             for a in v["after"]:
                 needed[a].append((s, 0.0))
             for u in v["recv"]:
-                needed[sender[u]].append((s, self.units[u]["blocks"] * block_bytes / LINK + HOP_US))
+                unit = self.units[u]
+                needed[sender[u]].append((s, unit["blocks"] * block_bytes / LINK + HOP_US + FAR_US * (unit["far"] - 1)))
         path = {}
 
         def length(s):
@@ -88,8 +99,9 @@
                 if any(a not in done for a in v["after"]) or any(u not in arrival for u in v["recv"]):
                     continue
                 ready = max([done[a] for a in v["after"]] + [arrival[u] for u in v["recv"]] + [core])
-                begin = max([ready] + [links.get(self.units[u]["link"], 0.0) - AHEAD_US for u in v["send"]])
-                key = (round(begin / 0.2), v["wave"], -path[s])
+                ahead = AHEAD_US if v["wave"] == 0 else LATER_US[0]
+                begin = max([ready] + [links.get(self.units[u]["link"], 0.0) - ahead for u in v["send"]])
+                key = (round((begin + LATER_US[1] * min(v["wave"], 1)) / 0.2), v["wave"], -path[s])
                 if best is None or key < best[0]:
                     best = (key, s, ready)
             _, s, ready = best
@@ -100,22 +112,23 @@
             for u in self.steps[s]["send"]:
                 link = self.units[u]["link"]
                 rate = LINK if link[0] != "core" else 8 * LINK
+                far = self.units[u]["far"]
                 begin = max(core, links.get(link, 0.0))
-                links[link] = begin + self.units[u]["blocks"] * block_bytes / rate
-                arrival[u] = links[link] + HOP_US
+                links[link] = begin + self.units[u]["blocks"] * far * block_bytes / rate
+                arrival[u] = links[link] + HOP_US + FAR_US * (far - 1)
         self.total = core
         return result
 
 
 def need_order():
     blocks, where, seg = [], {}, []
-    for wave in range(len(STREAMS) // 2):
-        pair = [2 * wave, 2 * wave + 1]
+    for wave in range(max(WAVES) + 1):
+        pair = [st for st in range(len(STREAMS)) if WAVES[st] == wave]
         rest = {st: [(off, sub) for off in offsets(sizes(STREAMS[st])[0]) for sub in range(subs_of(STREAMS[st]))] for st in pair}
-        if NX > 1:
-            for st in pair:
-                n = sizes(STREAMS[st])[0]
-                rank = {o: min(o, n - o) for o in range(n)}
+        for st in pair:
+            n = sizes(STREAMS[st])[0]
+            rank = {o: min(o, n - o) for o in range(n)}
+            if STREAMS[st] == "x":
                 rest[st].sort(key=lambda u: (u[0] == 0, (rank[u[0]] != n // 2) * u[1], -rank[u[0]]))
         slots = 5
         for t in range(slots):
@@ -135,9 +148,9 @@
     return blocks, where, seg
 
 
-def kernel(plan_only, group, table, lists, readers, seq, features, tiles, weight, hidden, ghosts, *scratch):
-    feats, bank, mix, part, gy, g, send_sem, recv_sem, local_sem = scratch[:9]
-    per = [scratch[9 + 5 * st:14 + 5 * st] for st in range(len(STREAMS))]
+def kernel(plan_only, group, used, table, lists, readers, seq, features, tiles, weight, hidden, ghosts, *scratch):
+    feats, bank, mix, part, gy, g, gx, mixed, send_sem, recv_sem, local_sem = scratch[:11]
+    per = [scratch[11 + 5 * st:16 + 5 * st] for st in range(len(STREAMS))]
     blocks, where, seg = need_order()
     plan = Plan()
     size = features.shape[1]
@@ -148,12 +161,16 @@
         edge, feat = lax.axis_index("edge"), lax.axis_index("feat")
         x, z, y, core = edge // NZ, edge % NZ, feat // NC, feat % NC
         peers = {}
-        for s in SIGNS:
-            peers["x", s] = (((x + s + NX) % NX) * NZ + z, feat)
-            peers["z", s] = (x * NZ + (z + s + NZ) % NZ, feat)
-            peers["y", s] = (edge, ((y + s + NY) % NY) * NC + core)
-        peers["core", 1] = (edge, y * NC + (core + 1) % NC)
-        greeted = [k for k in peers if {"x": NX, "z": NZ, "y": NY, "core": NC}[k[0]] > 1]
+        for axis, by in used:
+            if axis == "x":
+                peers[axis, by] = ((x + by) % NX * NZ + z, feat)
+            elif axis == "z":
+                peers[axis, by] = (x * NZ + (z + by) % NZ, feat)
+            elif axis == "y":
+                peers[axis, by] = (edge, (y + by) % NY * NC + core)
+            else:
+                peers[axis, by] = (edge, y * NC + (core + by) % NC)
+        greeted = list(peers)
         barrier = pltpu.get_barrier_semaphore()
         for k in greeted:
             pl.semaphore_signal(barrier, inc=1, device_id=peers[k], device_id_type=MESH_ID)
@@ -170,13 +187,17 @@
                     local_sem.at[2 + ry],
                 )
             )
+        for c in range(4):
+            loads.append(pltpu.make_async_copy(features.at[pl.ds(c * rows, rows)], gx.at[c, 0, 0], local_sem.at[2 + NY + c]))
         for c in loads:
             c.start()
         bank[deep] = jnp.zeros_like(bank[deep])
         loads[0].wait()
         loads[1].wait()
-
-    def products(lo, hi):
+        for c in loads[2 + NY:]:
+            c.wait()
+
+    def products(lo, hi, source):
         def body(i, carry):
             parts = []
             for b in range(group):
@@ -188,14 +209,18 @@
                     slot = slot + jnp.where(lists[owner * 4 + c] == j, c, 0)
                 base = (owner * 4 + slot % 4) * 4
                 parts.append(jnp.concatenate([bank[table[base + c]] for c in range(4)], axis=1))
-            value = jnp.dot(jnp.concatenate(parts, axis=0), feats[...], preferred_element_type=jnp.float32)
+            value = jnp.dot(jnp.concatenate(parts, axis=0), source[...], preferred_element_type=jnp.float32)
             part[pl.ds(i * group, group)] = value.reshape(group, rows, size)
             return carry
 
         lax.fori_loop(lo // group, hi // group, body, 0)
 
     for t, (wave, lo, hi) in enumerate(seg):
-        plan.step(("P", t), functools.partial(products, lo, hi), cost=GROUP_US * (hi - lo) / 4, after=[("P", t - 1)] if t else [], wave=wave)
+        pre = PRE[WAVES.index(wave)]
+        plan.step(
+            ("P", t), functools.partial(products, lo, hi, mixed if pre else feats), cost=GROUP_US * (hi - lo) / 4,
+            after=([("P", t - 1)] if t else []) + ([("V", c) for c in range(4)] if pre else []), wave=wave,
+        )
 
     def cut(half):
         return pl.ds(half * mid, mid)
@@ -211,9 +236,51 @@
 
         lax.fori_loop(0, count, body, 0) if count > 1 else body(0, 0)
 
+    def rows_of(s, d, n):
+        hv = halves_of(s, d + 1, n)
+        return pl.ds(hv[0] * mid, mid * len(hv)), len(hv) / 2
+
+    def all_columns(key, ref, i, ready, wave):
+        hy, arrivals = NY // 2, []
+        if NC > 1:
+            plan.unit(("YP", key, 0, 0), ("core", 1), 1, (ref, (i, 0, 0)), (ref, (i, 0, 1)))
+            arrivals.append(("YP", key, 0, 0))
+        for s in SIGNS:
+            for d in range(hy):
+                w, c = rows_of(s, d, NY)
+                here, there = -s * d % NY, -s * (d + 1) % NY
+                plan.unit(("Y", key, s, d), ("y", s), c, (ref, (i, here, 0, w)), (ref, (i, there, 0, w)))
+                arrivals.append(("Y", key, s, d))
+                if NC > 1:
+                    plan.unit(("YP", key, s, d + 1), ("core", 1), c, (ref, (i, there, 0, w)), (ref, (i, there, 1, w)))
+                    arrivals.append(("YP", key, s, d + 1))
+        send = ([("Y", key, s, 0) for s in SIGNS] if NY > 1 else []) + ([("YP", key, 0, 0)] if NC > 1 else [])
+        plan.step(("Y", key), after=ready, send=send, wave=wave)
+        for s in SIGNS:
+            for d in range(1, hy + 1):
+                send = ([("Y", key, s, d)] if d < hy else []) + ([("YP", key, s, d)] if NC > 1 else [])
+                plan.step(("Y", key, s, d), recv=[("Y", key, s, d - 1)], send=send, wave=wave)
+        return arrivals
+
+    def by_weight(ref, i, put):
+        def wide(swap):
+            order = [(ry, (rc + swap) % NC) for ry in range(NY) for rc in range(NC)]
+            put(jnp.dot(jnp.concatenate([ref[i, ry, rc] for ry, rc in order], axis=1), mix[...], preferred_element_type=jnp.float32))
+
+        for c in range(NC):
+            pl.when(core == c)(functools.partial(wide, c))
+
+    for c in range(4) if any(PRE) else ():
+        arrivals = all_columns(("X", c), gx, c, [("P", 0)], 0)
+
+        def put(value, c=c):
+            mixed[pl.ds(c * rows, rows)] = value.astype(jnp.bfloat16)
+
+        plan.step(("V", c), functools.partial(by_weight, gx, c, put), after=[("W",), ("Y", ("X", c))], recv=arrivals, cost=0.5)
+
     everything = []
     for st, kind in enumerate(STREAMS):
-        wave = st // 2
+        wave = WAVES[st]
         n1, n2 = sizes(kind)
         a1, a2 = ("z", "x") if kind == "z" else ("x", "z")
         h1, h2, hy = n1 // 2, n2 // 2, NY // 2
@@ -268,94 +335,106 @@
                 recv=[("A", st, s, 1, sub) for s in SIGNS] if n1 > 1 else [], cost=0.15, wave=wave,
             )
 
-        def unit2(s, r, ref, n2=n2):
-            hv = halves_of(s, r, n2)
-            return ref, (lead(s), r - 1, pl.ds(hv[0] * mid, mid * len(hv)))
-
-        for s in SIGNS:
-            for r in range(1, h2 + 1):
-                plan.unit(("B", st, s, r), (a2, s), len(halves_of(s, r, n2)) / 2, unit2(s, r, s2), unit2(s, r, r2))
-
-        def in2(s, r, k, half, r2=r2):
-            return r2[lead(s), r - 1, cut(half)]
-
-        for s in SIGNS:
-            for r in range(h2, 0, -1):
-                p = off2.index(s * r % n2)
+        if a2 in DIRECT["B"]:
+            for o in off2[:-1]:
+                plan.unit(("B", st, o), (a2, o), 1, (s2, (o - 1,)), (r2, (o - 1,)))
+                p = off2.index(o)
 
                 def own(k, half, p=p, q=q):
                     return q[p, cut(half)]
 
-                def put(k, half, value, s=s, r=r, s2=s2):
-                    s2[lead(s), r - 1, cut(half)] = value.astype(jnp.bfloat16)
-
-                extras = [
-                    (half, [functools.partial(in2, s, r + 1)] if half in halves_of(s, r + 1, n2) else []) for half in halves_of(s, r, n2)
-                ]
+                def put(k, half, value, o=o, s2=s2):
+                    s2[o - 1, cut(half)] = value.astype(jnp.bfloat16)
+
                 plan.step(
-                    ("B", st, s, r), functools.partial(total, 1, own, extras, put), after=[("Af", st, p // width)],
-                    recv=[("B", st, s, r + 1)] if r < h2 else [], send=[("B", st, s, r)], cost=0.06, wave=wave,
+                    ("B", st, o), functools.partial(total, 1, own, [(0, []), (1, [])], put), after=[("Af", st, p // width)],
+                    send=[("B", st, o)], cost=0.06, wave=wave,
                 )
+
+            def come(o, k, half, r2=r2):
+                return r2[o - 1, cut(half)]
+
+            last = [(half, [functools.partial(come, o) for o in off2[:-1]]) for half in (0, 1)]
+            last_recv = [("B", st, o) for o in off2[:-1]]
+        else:
+            def unit2(s, r, ref, n2=n2):
+                hv = halves_of(s, r, n2)
+                return ref, (lead(s), r - 1, pl.ds(hv[0] * mid, mid * len(hv)))
+
+            for s in SIGNS:
+                for r in range(1, h2 + 1):
+                    plan.unit(("B", st, s, r), (a2, s), len(halves_of(s, r, n2)) / 2, unit2(s, r, s2), unit2(s, r, r2))
+
+            def in2(s, r, k, half, r2=r2):
+                return r2[lead(s), r - 1, cut(half)]
+
+            for s in SIGNS:
+                for r in range(h2, 0, -1):
+                    p = off2.index(s * r % n2)
+
+                    def own(k, half, p=p, q=q):
+                        return q[p, cut(half)]
+
+                    def put(k, half, value, s=s, r=r, s2=s2):
+                        s2[lead(s), r - 1, cut(half)] = value.astype(jnp.bfloat16)
+
+                    extras = [
+                        (half, [functools.partial(in2, s, r + 1)] if half in halves_of(s, r + 1, n2) else []) for half in halves_of(s, r, n2)
+                    ]
+                    plan.step(
+                        ("B", st, s, r), functools.partial(total, 1, own, extras, put), after=[("Af", st, p // width)],
+                        recv=[("B", st, s, r + 1)] if r < h2 else [], send=[("B", st, s, r)], cost=0.06, wave=wave,
+                    )
+
+            last = [(half, [functools.partial(in2, s, 1) for s in SIGNS if half in halves_of(s, 1, n2)]) for half in (0, 1)]
+            last_recv = [("B", st, s, 1) for s in SIGNS] if n2 > 1 else []
         p = off2.index(0)
 
         def own(k, half, p=p, q=q):
             return q[p, cut(half)]
 
         def put(k, half, value, st=st):
-            gy[st, 0, 0, cut(half)] = value.astype(jnp.bfloat16)
-
-        extras = [(half, [functools.partial(in2, s, 1) for s in SIGNS if half in halves_of(s, 1, n2)]) for half in (0, 1)]
+            if PRE[st]:
+                value = jnp.maximum(value, 0.0).astype(jnp.bfloat16)
+                g[st * NX * NZ, cut(half)] = value
+                hidden[pl.ds(st * rows + half * mid, mid)] = value
+            else:
+                gy[st, 0, 0, cut(half)] = value.astype(jnp.bfloat16)
+
         plan.step(
-            ("Bf", st), functools.partial(total, 1, own, extras, put), after=[("Af", st, p // width)],
-            recv=[("B", st, s, 1) for s in SIGNS] if n2 > 1 else [], cost=0.06, wave=wave,
+            ("Bf", st), functools.partial(total, 1, own, last, put), after=[("Af", st, p // width)],
+            recv=last_recv, cost=0.06, wave=wave,
         )
 
-        def rows_of(s, d, n):
-            hv = halves_of(s, d + 1, n)
-            return pl.ds(hv[0] * mid, mid * len(hv)), len(hv) / 2
-
-        arrivals = []
-        if NC > 1:
-            plan.unit(("YP", st, 0, 0), ("core", 1), 1, (gy, (st, 0, 0)), (gy, (st, 0, 1)))
-            arrivals.append(("YP", st, 0, 0))
-        for s in SIGNS:
-            for d in range(hy):
-                w, c = rows_of(s, d, NY)
-                here, there = -s * d % NY, -s * (d + 1) % NY
-                plan.unit(("Y", st, s, d), ("y", s), c, (gy, (st, here, 0, w)), (gy, (st, there, 0, w)))
-                arrivals.append(("Y", st, s, d))
-                if NC > 1:
-                    plan.unit(("YP", st, s, d + 1), ("core", 1), c, (gy, (st, there, 0, w)), (gy, (st, there, 1, w)))
-                    arrivals.append(("YP", st, s, d + 1))
-        send = ([("Y", st, s, 0) for s in SIGNS] if NY > 1 else []) + ([("YP", st, 0, 0)] if NC > 1 else [])
-        plan.step(("Y", st), after=[("Bf", st)], send=send, wave=wave)
-        for s in SIGNS:
-            for d in range(1, hy + 1):
-                send = ([("Y", st, s, d)] if d < hy else []) + ([("YP", st, s, d)] if NC > 1 else [])
-                plan.step(("Y", st, s, d), recv=[("Y", st, s, d - 1)], send=send, wave=wave)
+        if not PRE[st]:
+            arrivals = all_columns(st, gy, st, [("Bf", st)], wave)
+
+        a1, a2 = (("z", "x"), ("x", "z"))[FIRST[st] == "x"]
+        n1, n2 = {"z": NZ, "x": NX}[a1], {"z": NZ, "x": NX}[a2]
+        h1, h2 = n1 // 2, n2 // 2
 
         def slot(qpos, q2, st=st, n1=n1):
             return st * NX * NZ + q2 * n1 + qpos
 
-        def mixing(st=st, slot=slot):
-            def wide(swap):
-                order = [(ry, (rc + swap) % NC) for ry in range(NY) for rc in range(NC)]
-                value = jnp.dot(
-                    jnp.concatenate([gy[st, ry, rc] for ry, rc in order], axis=1), mix[...], preferred_element_type=jnp.float32
-                )
-                value = jnp.maximum(value, 0.0).astype(jnp.bfloat16)
-                g[slot(0, 0)] = value
-                hidden[pl.ds(st * rows, rows)] = value
-
-            for c in range(NC):
-                pl.when(core == c)(functools.partial(wide, c))
-
-        plan.step(("H", st), mixing, after=[("W",), ("Y", st)], recv=arrivals, cost=0.7, wave=wave)
+        def finish(value, st=st):
+            value = jnp.maximum(value, 0.0).astype(jnp.bfloat16)
+            g[st * NX * NZ] = value
+            hidden[pl.ds(st * rows, rows)] = value
+
+        if PRE[st]:
+            plan.step(("H", st), after=[("Bf", st)], wave=wave)
+        else:
+            plan.step(
+                ("H", st), functools.partial(by_weight, gy, st, finish), after=[("W",), ("Y", st)], recv=arrivals, cost=0.5, wave=wave
+            )
 
         back1 = offsets(n1)[::-1]
         where1 = {o: i for i, o in enumerate(back1)}
         sets = groups_of(n1)
-        for s in SIGNS:
+        for o in range(1, n1) if a1 in DIRECT["C"] else ():
+            plan.unit(("C", st, o), (a1, o), 1, (g, (slot(0, 0),)), (g, (slot(where1[-o % n1], 0),)))
+            everything.append(("C", st, o))
+        for s in SIGNS if a1 not in DIRECT["C"] else ():
             for d in range(h1):
                 w, c = rows_of(s, d, n1)
                 plan.unit(
@@ -371,9 +450,15 @@
                     plan.unit(("D", st, i, s, d), (a2, s), c * len(members), (g, (here, w)), (g, (there, w)))
                     everything.append(("D", st, i, s, d))
         second = lambda i: [("D", st, i, s, 0) for s in SIGNS] if h2 else []
-        plan.step(("C", st), after=[("H", st)], send=[("C", st, s, 0) for s in SIGNS] if h1 else [], wave=wave)
+        if a1 in DIRECT["C"]:
+            far = sorted(range(1, n1), key=lambda o: -min(o, n1 - o))
+            plan.step(("C", st), after=[("H", st)], send=[("C", st, o) for o in far], wave=wave)
+            for d in range(1, h1 + 1):
+                plan.step(("D", st, d), recv=[("C", st, o) for o in sorted({d, n1 - d})], send=second(d), wave=wave)
+        else:
+            plan.step(("C", st), after=[("H", st)], send=[("C", st, s, 0) for s in SIGNS] if h1 else [], wave=wave)
         plan.step(("D", st, 0), after=[("H", st)], send=second(0), wave=wave)
-        for d in range(1, h1 + 1):
+        for d in range(1, h1 + 1) if a1 not in DIRECT["C"] else ():
             for s in SIGNS:
                 if d < h1:
                     plan.step(("C", st, s, d), recv=[("C", st, s, d - 1)], send=[("C", st, s, d)], wave=wave)
@@ -384,10 +469,10 @@
                     plan.step(("D", st, i, s, d), recv=[("D", st, i, s, d - 1)], send=[("D", st, i, s, d)], wave=wave)
 
     def weights():
-        for c in loads[2:]:
+        for c in loads[2:2 + NY]:
             c.wait()
 
-    plan.step(("W",), weights, after=[("P", len(seg) - 1)])
+    plan.step(("W",), weights, after=[("P", 0)])
 
     def place(q, n):
         return jnp.where(2 * q < n, 2 * q, 2 * (n - q) - 1) % n
@@ -397,7 +482,11 @@
             v = readers[r]
             o, j = v // 4, v % 4
             rx, rz = (o // NZ - x + NX) % NX, (o % NZ - z + NZ) % NZ
-            at = j * NX * NZ + jnp.where(j % 2 == 0, rx * NZ + place(rz, NZ), rz * NX + place(rx, NX))
+            first_z = j < 0
+            for st, axis in enumerate(FIRST):
+                if axis == "z":
+                    first_z = jnp.logical_or(first_z, j == st)
+            at = j * NX * NZ + jnp.where(first_z, rx * NZ + place(rz, NZ), rz * NX + place(rx, NX))
             ghosts[pl.ds(pl.multiple_of(r * rows, rows), rows)] = g[at]
             return carry
 
@@ -414,7 +503,7 @@
         (sref, sat), (dref, dat) = u["src"], u["dst"]
         return pltpu.make_async_remote_copy(
             src_ref=sref.at[sat], dst_ref=dref.at[dat], send_sem=send_sem.at[u["index"]], recv_sem=recv_sem.at[u["index"]],
-            device_id=peers[u["link"]], device_id_type=MESH_ID,
+            device_id=peers[u["to"]], device_id_type=MESH_ID,
         )
 
     copies = {name: copy(name) for name in plan.units}
@@ -444,11 +533,14 @@
     shapes = [
         v((4 * rows, size), bf), v((deep + 1, rows, rows), bf), v((NY * NC * size, size), bf), v((len(blocks), rows, size), fp),
         v((len(STREAMS), NY, NC, rows, size), bf), v((len(STREAMS) * NX * NZ, rows, size), bf),
-        pltpu.SemaphoreType.DMA((count,)), pltpu.SemaphoreType.DMA((count,)), pltpu.SemaphoreType.DMA((2 + NY,)),
+        v((4, NY, NC, rows, size), bf), v((4 * rows, size), bf),
+        pltpu.SemaphoreType.DMA((count,)), pltpu.SemaphoreType.DMA((count,)), pltpu.SemaphoreType.DMA((6 + NY,)),
     ]
     for kind in STREAMS:
         n1, n2 = sizes(kind)
         first, second = v((2, max(n1 // 2, 1), n2, rows, size), bf), v((2, max(n2 // 2, 1), rows, size), bf)
+        if {"z": "x", "x": "z"}[kind] in DIRECT["B"]:
+            second = v((max(n2 - 1, 1), rows, size), bf)
         shapes += [first, first, second, second, v((n2, rows, size), fp)]
     return shapes
 
@@ -466,12 +558,13 @@
     pair = tile_slot * 4 + tile_col
     table = deep + jnp.sum(jnp.where(keys[:, None] == pair[None, :], tile_id[None, :] - deep, 0), axis=1)
     args = (table.astype(jnp.int32), lists, readers, seq, features, tiles, weight)
-    plan, order = kernel(True, group, *args, None, None, *([None] * 29))
+    plan, order = kernel(True, group, None, *args, None, None, *([None] * 31))
+    used = sorted({u["to"] for u in plan.units.values()} | {(u["to"][0], -u["to"][1] % {"x": NX, "z": NZ, "y": NY, "core": NC}[u["to"][0]]) for u in plan.units.values()})
     vmem = pl.BlockSpec(memory_space=pltpu.VMEM)
     smem = pl.BlockSpec(memory_space=pltpu.SMEM)
     hbm = pl.BlockSpec(memory_space=pltpu.HBM)
     return pl.pallas_call(
-        functools.partial(kernel, False, group),
+        functools.partial(kernel, False, group, used),
         out_shape=(
             jax.ShapeDtypeStruct(features.shape, jnp.bfloat16),
             jax.ShapeDtypeStruct((readers.shape[0] * block, size), jnp.bfloat16),
@@ -479,7 +572,7 @@
         in_specs=[smem, smem, smem, smem, hbm, hbm, hbm],
         out_specs=(vmem, vmem),
         scratch_shapes=scratch_shapes(block, size, deep, len(plan.units)),
-        compiler_params=pltpu.CompilerParams(collective_id=0, has_side_effects=True, vmem_limit_bytes=60 << 20),
+        compiler_params=pltpu.CompilerParams(collective_id=0, has_side_effects=True, vmem_limit_bytes=52 << 20),
         name="layer",
     )(*args)
 

time: 107 us -> 98.4 us (0.920)
  Pallas kernels: 99.8 us -> 90.8 us
    pallas_call x1, Pallas kernels: 99.8 us -> 90.8 us  [local(): pl.pallas_call(functools.partial(kernel, False, group, used), out_shape=(...]
    unnamed x4 -> x12, local copies, waits for them, and re-layouts: 4.27 us -> 5.54 us
where the time goes in v3:
time: 98.4 us; the launch traced here: 98.1 us
  Pallas kernels  90.8 us (92%)
  local copies, waits for them, and re-layouts  5.73 us (6%)
    pallas_call x1, Pallas kernels, local(): pl.pallas_call(functools.partial(kernel, False, group, used), out_shape=(...  90.8 us
    unnamed x12, local copies, waits for them, and re-layouts  5.54 us

profile of v3, /device:TPU:8, one launch (start us, length us, event | category | flops | bytes accessed | tf_op | source)
XLA Modules:
  0.0 98.1 jit_solution(2250133601607568718)
XLA Ops:
  0.6 0.0 copy-start
  0.6 0.8 copy-done
  1.5 0.7 multiply_add_fusion
  2.2 0.2 select_reduce_fusion
  2.4 0.1 copy.13
  2.5 0.1 reshape.11.lists
  2.6 0.0 copy-start.1
  2.6 1.0 %copy-done.1 = bf16[2048,128]{1,0:T(8,128)(2,1)S(1)} copy-done((bf16[2048,128]{1,0:T(8,128)(2,1)S(1)}, bf16[2048,128]{1,0:T(8,128)(2,1)}, u32[]{:S(2)}) %copy-start.1) | copy-done | bytes 524312
  3.6 0.0 copy-start.2
  3.6 0.9 copy-done.2
  4.5 0.0 copy-start.3
  4.5 0.7 copy-done.3
  5.2 0.0 copy-start.4
  5.2 0.7 copy-done.4
  5.8 90.8 %layer.1 = (bf16[512,128]{1,0:T(8,128)(2,1)S(1)}, bf16[2048,128]{1,0:T(8,128)(2,1)S(1)}) custom-call(s32[512]{0:T(512)S(1)} %broadcast_add_fusion.table, s32[128]{0:T(128)S(1)} %reshape.11.lists, s32[16]{0:T(128)S(1)} %copy-done.3, s32[128]{0:T(128)S(1)} %copy-done.4, bf16[512,128]{1,0:T(8,128)(2,1)S(1)} %copy-done.2, bf16[48,128,128]{2,1,0:T(8,128)(2,1)} %tiles.1, ...), custom_call_target="tpu_custom_call" | custom-call | tf_op jit(solution)/shard_map/layer/pallas_call | solution.py:566
  96.7 0.7 copy.16
  97.3 0.8 copy.17
  (2 shorter events, 0.0 us)
Async XLA Ops:
  0.6 0.8 copy-start
  2.6 1.0 %copy-start.1 = (bf16[2048,128]{1,0:T(8,128)(2,1)S(1)}, bf16[2048,128]{1,0:T(8,128)(2,1)}, u32[]{:S(2)}) copy-start(bf16[2048,128]{1,0:T(8,128)(2,1)} %weight.1) | copy-start | bytes 1572868
  3.6 0.9 copy-start.2
  4.5 0.7 copy-start.3
  5.2 0.7 copy-start.4

commit v4 on v3

--- a/solution.py
+++ b/solution.py
@@ -12,9 +12,9 @@
 STREAMS = ("x", "z", "x", "z")
 PRE = (False, False, True, True)
 WAVES = (0, 0, 1, 1)
-FIRST = ('z', 'x', 'z', 'x')
+FIRST = ('x', 'z', 'x', 'z')
 DIRECT = {"B": (), "C": (), "Y": False}
-SUBS = {"z": 2, "x": 4}
+SUBS = {'z': 2, 'x': 4}
 HOP_US, LINK, GROUP_US, AHEAD_US, FAR_US = 2.3, 46.5e3, 0.3, 0.5, 0.8
 LATER_US = (1.5, 0.0)
 MESH_ID = pl.DeviceIdType.MESH
@@ -130,7 +130,7 @@
             rank = {o: min(o, n - o) for o in range(n)}
             if STREAMS[st] == "x":
                 rest[st].sort(key=lambda u: (u[0] == 0, (rank[u[0]] != n // 2) * u[1], -rank[u[0]]))
-        slots = 5
+        slots = 8
         for t in range(slots):
             begin = len(blocks)
             for st in pair:

time: 98.4 us -> 97 us (0.986)
  Pallas kernels: 90.8 us -> 89.4 us
    pallas_call x1, Pallas kernels: 90.8 us -> 89.4 us  [local(): pl.pallas_call(functools.partial(kernel, False, group, used), out_shape=(...]
where the time goes in v4:
time: 97 us; the launch traced here: 96.7 us
  Pallas kernels  89.4 us (92%)
  local copies, waits for them, and re-layouts  5.73 us (6%)
    pallas_call x1, Pallas kernels, local(): pl.pallas_call(functools.partial(kernel, False, group, used), out_shape=(...  89.4 us
    unnamed x12, local copies, waits for them, and re-layouts  5.54 us

profile of v4, /device:TPU:8, one launch (start us, length us, event | category | flops | bytes accessed | tf_op | source)
XLA Modules:
  0.0 96.7 jit_solution(17884485750294175828)
XLA Ops:
  0.6 0.0 copy-start
  0.6 0.8 copy-done
  1.5 0.7 multiply_add_fusion
  2.2 0.2 select_reduce_fusion
  2.4 0.1 copy.13
  2.5 0.1 reshape.11.lists
  2.6 0.0 copy-start.1
  2.6 1.0 %copy-done.1 = bf16[2048,128]{1,0:T(8,128)(2,1)S(1)} copy-done((bf16[2048,128]{1,0:T(8,128)(2,1)S(1)}, bf16[2048,128]{1,0:T(8,128)(2,1)}, u32[]{:S(2)}) %copy-start.1) | copy-done | bytes 524312
  3.6 0.0 copy-start.2
  3.6 0.9 copy-done.2
  4.5 0.0 copy-start.3
  4.5 0.7 copy-done.3
  5.2 0.0 copy-start.4
  5.2 0.7 copy-done.4
  5.8 89.4 %layer.1 = (bf16[512,128]{1,0:T(8,128)(2,1)S(1)}, bf16[2048,128]{1,0:T(8,128)(2,1)S(1)}) custom-call(s32[512]{0:T(512)S(1)} %broadcast_add_fusion.table, s32[128]{0:T(128)S(1)} %reshape.11.lists, s32[16]{0:T(128)S(1)} %copy-done.3, s32[128]{0:T(128)S(1)} %copy-done.4, bf16[512,128]{1,0:T(8,128)(2,1)S(1)} %copy-done.2, bf16[48,128,128]{2,1,0:T(8,128)(2,1)} %tiles.1, ...), custom_call_target="tpu_custom_call" | custom-call | tf_op jit(solution)/shard_map/layer/pallas_call | solution.py:566
  95.2 0.7 copy.16
  95.9 0.8 copy.17
  (2 shorter events, 0.0 us)
Async XLA Ops:
  0.6 0.8 copy-start
  2.6 1.0 %copy-start.1 = (bf16[2048,128]{1,0:T(8,128)(2,1)S(1)}, bf16[2048,128]{1,0:T(8,128)(2,1)}, u32[]{:S(2)}) copy-start(bf16[2048,128]{1,0:T(8,128)(2,1)} %weight.1) | copy-start | bytes 1572868
  3.6 0.9 copy-start.2
  4.5 0.7 copy-start.3
  5.2 0.7 copy-start.4
